TPU v7x, 32 devices: a whole 2x2x4 slice. The times are simulated.
32 devices in a mesh: rep: 4 (over y, x), shard: 8 (over z, core).
Axes of the slice: x: 2, y: 2, z: 4, core: 2. Of those that a mesh axis runs over, the one named last changes fastest.
Arguments:
- hidden_in: float32 [4096, 768], P(('rep', 'shard')), may hold values from -6 to 6
- doc_ids: int32 [32, 128], P(('rep', 'shard')), may hold values from 0 to 3, never falling along the last dimension, each value on 1 to 64 neighbouring positions
- cotangent: float32 [4096, 768], P(('rep', 'shard')), may hold values from -6 to 6
- pre_gain: float32 [1, 768], P(None, 'shard'), may hold values from 0.25 to 1.75
- pre_shift: float32 [1, 768], P(None, 'shard'), may hold values from -3 to 3
- qkv_weight: float32 [1, 768, 2304], P(None, 'shard'), may hold values from -0.21875 to 0.21875
- query_bias: float32 [1, 768], P(None, 'shard'), may hold values from -3 to 3
- value_bias: float32 [1, 768], P(None, 'shard'), may hold values from -3 to 3
- out_weight: float32 [1, 768, 768], P(None, 'shard'), may hold values from -0.875 to 0.875
- out_bias: float32 [1, 768], P(None, 'shard'), may hold values from -3 to 3
- post_gain: float32 [1, 768], P(None, 'shard'), may hold values from 0.25 to 1.75
- post_shift: float32 [1, 768], P(None, 'shard'), may hold values from -3 to 3
- up_weight: float32 [1, 768, 3072], P(None, 'shard'), may hold values from -0.21875 to 0.21875
- up_bias: float32 [1, 3072], P(None, 'shard'), may hold values from -3 to 3
- down_weight: float32 [1, 3072, 768], P(None, 'shard'), may hold values from -0.109375 to 0.109375
- down_bias: float32 [1, 768], P(None, 'shard'), may hold values from -3 to 3
Outputs:
- hidden_out: float32 [4096, 768], P(('rep', 'shard'))
- input_grad: float32 [4096, 768], P(('rep', 'shard'))
- grad_pre_gain: float32 [1, 768], P(None, 'shard')
- grad_pre_shift: float32 [1, 768], P(None, 'shard')
- grad_qkv_weight: float32 [1, 768, 2304], P(None, 'shard')
- grad_query_bias: float32 [1, 768], P(None, 'shard')
- grad_value_bias: float32 [1, 768], P(None, 'shard')
- grad_out_weight: float32 [1, 768, 768], P(None, 'shard')
- grad_out_bias: float32 [1, 768], P(None, 'shard')
- grad_post_gain: float32 [1, 768], P(None, 'shard')
- grad_post_shift: float32 [1, 768], P(None, 'shard')
- grad_up_weight: float32 [1, 768, 3072], P(None, 'shard')
- grad_up_bias: float32 [1, 3072], P(None, 'shard')
- grad_down_weight: float32 [1, 3072, 768], P(None, 'shard')
- grad_down_bias: float32 [1, 768], P(None, 'shard')
Inputs may be any that keep to these rules, and one draw needn't show every extreme that they name: `doc_ids`: along each row the document number never falls; all 4 documents appear in every row, each of 1 to 64 tokens, one of exactly 64.
All inputs are finite; a program needn't handle non-finite values.
Results may differ from a plain program's by a relative error of at most 0.018.
Values may be sent and summed in bfloat16 or wider, within the bound.
No kernel may reach another device: no remote copies, remote signals or barrier semaphores. Data moves between devices by JAX's collectives and lax.ppermute only.
A program may use at most 128 MiB of HBM per device.

v0:
```python
import jax
import jax.numpy as jnp
from jax import lax
from jax.sharding import PartitionSpec as P

HEADS = 12
HEAD = 64
LAYERS = 1


EPS = 1e-05
GELU_C = 0.7978845608028654
NEG_FILL = -1e30


def norm(values_in, gains, shifts):
    average = jnp.mean(values_in, axis=-1, keepdims=True)
    centred = values_in - average
    spread = jnp.mean(centred * centred, axis=-1, keepdims=True)
    return centred * lax.rsqrt(spread + EPS) * gains + shifts


def gelu_tanh(values_in):
    return (
        0.5
        * values_in
        * (1.0 + jnp.tanh(GELU_C * (values_in + 0.044715 * values_in * values_in * values_in)))
    )


def project(left, right):
    return jnp.dot(left, right, preferred_element_type=jnp.float32)


def project_back(left, right):
    return lax.dot_general(
        left, right, (((0,), (0,)), ((), ())), preferred_element_type=jnp.float32
    )


def project_trans(left, right):
    return lax.dot_general(
        left, right, (((1,), (1,)), ((), ())), preferred_element_type=jnp.float32
    )


def layer_slices(shards, layer_index):
    return tuple((stacked[layer_index].astype(jnp.bfloat16) for stacked in shards))


def fetch_forward(shards, layer_index):
    parts = layer_slices(shards, layer_index)
    return (
        lax.all_gather(parts[0], "shard", axis=0, tiled=True),
        lax.all_gather(parts[1], "shard", axis=0, tiled=True),
        lax.all_gather(parts[2], "shard", axis=0, tiled=True),
        lax.all_gather(parts[3], "shard", axis=0, tiled=True),
        lax.all_gather(parts[4], "shard", axis=0, tiled=True),
        lax.all_gather(parts[5], "shard", axis=0, tiled=True),
        lax.all_gather(parts[6], "shard", axis=0, tiled=True),
        lax.all_gather(parts[7], "shard", axis=0, tiled=True),
        lax.all_gather(parts[8], "shard", axis=0, tiled=True),
        lax.all_gather(parts[9], "shard", axis=0, tiled=True),
        lax.all_gather(parts[10], "shard", axis=0, tiled=True),
        lax.all_gather(parts[11], "shard", axis=0, tiled=True),
        lax.all_gather(parts[12], "shard", axis=0, tiled=True),
    )


def reduce_nested_rest(grads):
    owned = (
        lax.psum_scatter(
            grads[0].astype(jnp.bfloat16), "shard", scatter_dimension=0, tiled=True
        ).astype(jnp.float32),
        lax.psum_scatter(
            grads[1].astype(jnp.bfloat16), "shard", scatter_dimension=0, tiled=True
        ).astype(jnp.float32),
        lax.psum_scatter(
            grads[2].astype(jnp.bfloat16), "shard", scatter_dimension=0, tiled=True
        ).astype(jnp.float32),
        lax.psum_scatter(
            grads[3].astype(jnp.bfloat16), "shard", scatter_dimension=0, tiled=True
        ).astype(jnp.float32),
        lax.psum_scatter(
            grads[4].astype(jnp.bfloat16), "shard", scatter_dimension=0, tiled=True
        ).astype(jnp.float32),
        lax.psum_scatter(
            grads[5].astype(jnp.bfloat16), "shard", scatter_dimension=0, tiled=True
        ).astype(jnp.float32),
        lax.psum_scatter(
            grads[6].astype(jnp.bfloat16), "shard", scatter_dimension=0, tiled=True
        ).astype(jnp.float32),
        lax.psum_scatter(
            grads[7].astype(jnp.bfloat16), "shard", scatter_dimension=0, tiled=True
        ).astype(jnp.float32),
        lax.psum_scatter(
            grads[8].astype(jnp.bfloat16), "shard", scatter_dimension=0, tiled=True
        ).astype(jnp.float32),
        lax.psum_scatter(
            grads[9].astype(jnp.bfloat16), "shard", scatter_dimension=0, tiled=True
        ).astype(jnp.float32),
        lax.psum_scatter(
            grads[10].astype(jnp.bfloat16), "shard", scatter_dimension=0, tiled=True
        ).astype(jnp.float32),
    )
    return (
        lax.psum(owned[0].astype(jnp.bfloat16), "rep").astype(jnp.float32),
        lax.psum(owned[1].astype(jnp.bfloat16), "rep").astype(jnp.float32),
        lax.psum(owned[2].astype(jnp.bfloat16), "rep").astype(jnp.float32),
        lax.psum(owned[3].astype(jnp.bfloat16), "rep").astype(jnp.float32),
        lax.psum(owned[4].astype(jnp.bfloat16), "rep").astype(jnp.float32),
        lax.psum(owned[5].astype(jnp.bfloat16), "rep").astype(jnp.float32),
        lax.psum(owned[6].astype(jnp.bfloat16), "rep").astype(jnp.float32),
        lax.psum(owned[7].astype(jnp.bfloat16), "rep").astype(jnp.float32),
        lax.psum(owned[8].astype(jnp.bfloat16), "rep").astype(jnp.float32),
        lax.psum(owned[9].astype(jnp.bfloat16), "rep").astype(jnp.float32),
        lax.psum(owned[10].astype(jnp.bfloat16), "rep").astype(jnp.float32),
    )


def block_scores(query_block, key_rows, doc_block, doc_row, offset):
    query_places = offset + lax.iota(jnp.int32, query_block.shape[0])
    key_places = lax.iota(jnp.int32, key_rows.shape[0])
    allowed = (query_places[:, None] >= key_places[None, :]) & (
        doc_block[:, None] == doc_row[None, :]
    )
    scores = (
        jnp.einsum("qhe,khe->hqk", query_block, key_rows, preferred_element_type=jnp.float32)
        * 0.125
    )
    return jnp.where(allowed[None], scores, NEG_FILL)


def attention_forward(queries, key_rows, value_rows, doc_row):
    length = queries.shape[0]
    rows_block = min(length, 512)
    blocks = length // rows_block

    def one_block(block_index):
        offset = block_index * rows_block
        scores = block_scores(queries, key_rows, doc_row, doc_row, offset)
        highest = jnp.max(scores, axis=-1, keepdims=True)
        log_total = highest + jnp.log(jnp.sum(jnp.exp(scores - highest), axis=-1, keepdims=True))
        weights = jnp.exp(scores - log_total).astype(jnp.bfloat16)
        mixed = jnp.einsum("hqk,khe->qhe", weights, value_rows, preferred_element_type=jnp.float32)
        return (mixed.astype(jnp.bfloat16), log_total)

    mixed, log_totals = lax.map(one_block, jnp.arange(blocks, dtype=jnp.int32))
    return (mixed.reshape(length, -1), log_totals)


def attention_backward(queries, key_rows, value_rows, doc_row, log_totals, grad_mixed):
    length = queries.shape[0]
    rows_block = min(length, 512)
    blocks = length // rows_block

    def one_block(carry, block_index):
        grad_keys, grad_values = carry
        offset = block_index * rows_block
        scores = block_scores(queries, key_rows, doc_row, doc_row, offset)
        weights = jnp.exp(scores - log_totals[block_index])
        grad_values = grad_values + jnp.einsum(
            "hqk,qhe->khe",
            weights.astype(jnp.bfloat16),
            grad_mixed,
            preferred_element_type=jnp.float32,
        )
        grad_weights = jnp.einsum(
            "qhe,khe->hqk", grad_mixed, value_rows, preferred_element_type=jnp.float32
        )
        grad_scores = weights * (
            grad_weights - jnp.sum(grad_weights * weights, axis=-1, keepdims=True)
        )
        grad_scores = grad_scores.astype(jnp.bfloat16)
        grad_query = (
            jnp.einsum("hqk,khe->qhe", grad_scores, key_rows, preferred_element_type=jnp.float32)
            * 0.125
        )
        grad_keys = (
            grad_keys
            + jnp.einsum("hqk,qhe->khe", grad_scores, queries, preferred_element_type=jnp.float32)
            * 0.125
        )
        return ((grad_keys, grad_values), grad_query)

    zeros_kv = jnp.zeros(key_rows.shape, jnp.float32)
    (grad_keys, grad_values), grad_queries = lax.scan(
        one_block, (zeros_kv, zeros_kv), jnp.arange(blocks, dtype=jnp.int32)
    )
    return (
        grad_queries.reshape(length, -1),
        grad_keys.reshape(length, -1),
        grad_values.reshape(length, -1),
    )


def layer_forward(hidden, weights, doc_row):
    (
        pre_gain,
        pre_shift,
        qkv_weight,
        query_bias,
        value_bias,
        out_weight,
        out_bias,
        post_gain,
        post_shift,
        up_weight,
        up_bias,
        down_weight,
        down_bias,
    ) = weights
    rows_here = hidden.shape[0]
    normed = norm(hidden, pre_gain.astype(jnp.float32), pre_shift.astype(jnp.float32)).astype(
        jnp.bfloat16
    )
    bias_row = jnp.concatenate([query_bias, jnp.zeros_like(query_bias), value_bias]).astype(
        jnp.float32
    )
    packed = (project(normed, qkv_weight) + bias_row).astype(jnp.bfloat16)
    shaped = packed.reshape(rows_here, 3, HEADS, HEAD)
    mixed, log_totals = attention_forward(shaped[:, 0], shaped[:, 1], shaped[:, 2], doc_row)
    middle = hidden + project(mixed, out_weight) + out_bias.astype(jnp.float32)
    normed_two = norm(middle, post_gain.astype(jnp.float32), post_shift.astype(jnp.float32)).astype(
        jnp.bfloat16
    )
    pre_act = project(normed_two, up_weight) + up_bias.astype(jnp.float32)
    activ = gelu_tanh(pre_act).astype(jnp.bfloat16)
    output = middle + project(activ, down_weight) + down_bias.astype(jnp.float32)
    stored = (hidden, normed, packed, mixed, log_totals, middle, normed_two, pre_act, activ)
    return (output, stored)


def layer_backward(grad_out, weights, stored, doc_row):
    (
        pre_gain,
        pre_shift,
        qkv_weight,
        query_bias,
        value_bias,
        out_weight,
        out_bias,
        post_gain,
        post_shift,
        up_weight,
        up_bias,
        down_weight,
        down_bias,
    ) = weights
    hidden, normed, packed, mixed, log_totals, middle, normed_two, pre_act, activ = stored
    rows_here, width = hidden.shape
    grad_down = grad_out.astype(jnp.bfloat16)
    activ_columns = lax.all_to_all(activ, "shard", split_axis=1, concat_axis=0, tiled=True)
    group_grads = lax.all_gather(grad_down, "shard", axis=0, tiled=True)
    grad_down_weight = project_back(activ_columns, group_grads)
    width_part = width // lax.axis_size("shard")
    column_total = jnp.sum(group_grads.astype(jnp.float32), axis=0)
    grad_down_bias = lax.dynamic_slice_in_dim(
        column_total, lax.axis_index("shard") * width_part, width_part, 0
    )
    grad_activ = project_trans(grad_down, down_weight)
    unused_gelu, gelu_pull = jax.vjp(gelu_tanh, pre_act)
    grad_pre = gelu_pull(grad_activ)[0].astype(jnp.bfloat16)
    grad_up_weight = project_back(normed_two, grad_pre)
    grad_up_bias = jnp.sum(grad_pre.astype(jnp.float32), axis=0)
    grad_normed_two = project_trans(grad_pre, up_weight)
    unused_post, post_pull = jax.vjp(
        norm, middle, post_gain.astype(jnp.float32), post_shift.astype(jnp.float32)
    )
    grad_middle, grad_post_gain, grad_post_shift = post_pull(grad_normed_two)
    grad_middle = grad_middle + grad_out
    grad_attn = grad_middle.astype(jnp.bfloat16)
    grad_out_weight = project_back(mixed, grad_attn)
    grad_out_bias = jnp.sum(grad_attn.astype(jnp.float32), axis=0)
    grad_mixed = (
        project_trans(grad_attn, out_weight).astype(jnp.bfloat16).reshape(rows_here, HEADS, HEAD)
    )
    shaped = packed.reshape(rows_here, 3, HEADS, HEAD)
    grad_queries, grad_keys, grad_values = attention_backward(
        shaped[:, 0], shaped[:, 1], shaped[:, 2], doc_row, log_totals, grad_mixed
    )
    grad_packed = jnp.concatenate([grad_queries, grad_keys, grad_values], axis=1).astype(
        jnp.bfloat16
    )
    grad_qkv_weight = project_back(normed, grad_packed)
    column_sums = jnp.sum(grad_packed.astype(jnp.float32), axis=0)
    grad_query_bias = column_sums[:width]
    grad_value_bias = column_sums[2 * width :]
    grad_normed = project_trans(grad_packed, qkv_weight)
    unused_pre, pre_pull = jax.vjp(
        norm, hidden, pre_gain.astype(jnp.float32), pre_shift.astype(jnp.float32)
    )
    grad_hidden, grad_pre_gain, grad_pre_shift = pre_pull(grad_normed)
    grads = (
        grad_pre_gain,
        grad_pre_shift,
        grad_qkv_weight,
        grad_query_bias,
        grad_value_bias,
        grad_out_weight,
        grad_out_bias,
        grad_post_gain,
        grad_post_shift,
        grad_up_weight,
        grad_up_bias,
        grad_down_weight,
        grad_down_bias,
    )
    return (grad_hidden + grad_middle, grads)


def on_device(
    hidden_in,
    doc_ids,
    cotangent,
    pre_gain,
    pre_shift,
    qkv_weight,
    query_bias,
    value_bias,
    out_weight,
    out_bias,
    post_gain,
    post_shift,
    up_weight,
    up_bias,
    down_weight,
    down_bias,
):
    shards = (
        pre_gain,
        pre_shift,
        qkv_weight,
        query_bias,
        value_bias,
        out_weight,
        out_bias,
        post_gain,
        post_shift,
        up_weight,
        up_bias,
        down_weight,
        down_bias,
    )
    doc_row = doc_ids[0]
    hidden = hidden_in
    layer_index = 0
    weights = fetch_forward(shards, layer_index)
    hidden, stored = layer_forward(hidden, weights, doc_row)
    gathered_all = [weights]
    stored_all = [stored]
    grad_flow = cotangent
    reduced_all = [None] * LAYERS
    for layer_index in reversed(range(LAYERS)):
        weights = gathered_all[layer_index]
        grad_flow, layer_grads = layer_backward(
            grad_flow, weights, stored_all[layer_index], doc_row
        )
        rest_grads = tuple((layer_grads[member] for member in range(11)))
        rest_sums = reduce_nested_rest(rest_grads)
        down_pair = (layer_grads[11], layer_grads[12])
        down_sums = (
            lax.psum(down_pair[0].astype(jnp.bfloat16), "rep").astype(jnp.float32),
            lax.psum(down_pair[1].astype(jnp.bfloat16), "rep").astype(jnp.float32),
        )
        reduced_all[layer_index] = tuple(rest_sums) + tuple(down_sums)
    stacked = tuple((jnp.stack([reduced_all[0][member]]) for member in range(13)))
    return (
        hidden,
        grad_flow,
        stacked[0],
        stacked[1],
        stacked[2],
        stacked[3],
        stacked[4],
        stacked[5],
        stacked[6],
        stacked[7],
        stacked[8],
        stacked[9],
        stacked[10],
        stacked[11],
        stacked[12],
    )


def solution(mesh):
    in_specs = (
        P(("rep", "shard"), None),
        P(("rep", "shard"), None),
        P(("rep", "shard"), None),
        P(None, "shard"),
        P(None, "shard"),
        P(None, "shard", None),
        P(None, "shard"),
        P(None, "shard"),
        P(None, "shard", None),
        P(None, "shard"),
        P(None, "shard"),
        P(None, "shard"),
        P(None, "shard", None),
        P(None, "shard"),
        P(None, "shard", None),
        P(None, "shard"),
    )
    out_specs = (
        P(("rep", "shard"), None),
        P(("rep", "shard"), None),
        P(None, "shard"),
        P(None, "shard"),
        P(None, "shard", None),
        P(None, "shard"),
        P(None, "shard"),
        P(None, "shard", None),
        P(None, "shard"),
        P(None, "shard"),
        P(None, "shard"),
        P(None, "shard", None),
        P(None, "shard"),
        P(None, "shard", None),
        P(None, "shard"),
    )
    return jax.shard_map(
        on_device, mesh=mesh, in_specs=in_specs, out_specs=out_specs, check_vma=False
    )
```

profile of v0, /device:TPU:0, one launch (start us, length us, event | category | flops | bytes accessed | tf_op | source)
XLA Modules:
  0.0 431.4 jit_solution(6924387649990992)
XLA Ops:
  7.2 2.1 convert_element_type.231
  9.4 0.7 convert_element_type.242
  10.2 0.9 convert_element_type.254
  11.3 0.9 convert_element_type.260
  12.2 0.7 convert_element_type.265
  13.2 0.6 fusion.54
  15.9 32.5 %all-reduce.17 = (bf16[768]{0:T(1024)(128)(2,1)S(1)}, bf16[768]{0:T(1024)(128)(2,1)S(1)}, bf16[768]{0:T(1024)(128)(2,1)S(1)}, bf16[768]{0:T(1024)(128)(2,1)S(1)}...) all-reduce(bf16[768]{0:T(1024)(128)(2,1)S(1)} %dynamic-update-slice, ...), channel_id=6, replica_groups=mesh['rep'=4,'shard'=8] {'shard'}, use_global_device_ids=true, to_apply=%add.3 | all-reduce | flops 5376 | bytes 21504 | tf_op jit(solution)/shard_map/all_gather | solution.py:58
  48.9 12.8 %all-gather.10 = bf16[1,3072]{1,0:T(2,128)(2,1)S(1)} all-gather(bf16[1,384]{1,0:T(2,128)(2,1)S(1)} %convert_element_type.256), channel_id=12, replica_groups=mesh['rep'=4,'shard'=8] {'shard'}, dimensions={1}, use_global_device_ids=true | all-gather | bytes 6912 | tf_op jit(solution)/shard_map/all_gather | solution.py:64
  61.8 2.8 fusion.11
  65.7 13.2 %all-gather.23.cloned.1.call-done = bf16[1,768,768]{2,1,0:T(8,128)(2,1)} async-done(((bf16[1,96,768]{2,1,0:T(8,128)(2,1)}), bf16[1,768,768]{2,1,0:T(8,128)(2,1)}) %all-gather.23.cloned.1.call-update) | async-done | bytes 1179664 | tf_op jit(solution)/shard_map/all_gather | solution.py:59
  78.9 1.7 fusion.56
  80.8 51.2 %all-gather.25.cloned.1.call-done = bf16[1,768,3072]{2,1,0:T(8,128)(2,1)} async-done(((bf16[1,96,3072]{2,1,0:T(8,128)(2,1)}), bf16[1,768,3072]{2,1,0:T(8,128)(2,1)}) %all-gather.25.cloned.1.call-update) | async-done | bytes 4718608 | tf_op jit(solution)/shard_map/all_gather | solution.py:63
  132.0 5.1 %multiply_convert_fusion = (bf16[128,3072]{1,0:T(8,128)(2,1)}, f32[128,3072]{1,0:T(8,128)}) fusion(f32[3072]{0:T(1024)S(1)} %bitcast.156, bf16[1,768,3072]{2,1,0:T(8,128)(2,1)} %all-gather.25.cloned.1.call-done, f32[128,768]{1,0:T(8,128)S(1)} %get-tuple-element.114, f32[768]{0:T(1024)S(1)} %convert_element_type.292, f32[768]{0:T(1024)S(1)} %convert_element_type.291, ...), kind=kOutput, calls=%fused_computation.27 | convolution fusion | flops 608403456 | bytes 7490560 | tf_op jit(solution)/shard_map/dot_general | solution.py:32
  137.1 47.0 %all-gather.27.cloned.1.call-done = bf16[1,3072,768]{2,1,0:T(8,128)(2,1)} async-done(((bf16[1,384,768]{2,1,0:T(8,128)(2,1)}), bf16[1,3072,768]{2,1,0:T(8,128)(2,1)}) %all-gather.27.cloned.1.call-update) | async-done | bytes 4718608 | tf_op jit(solution)/shard_map/all_gather | solution.py:65
  184.1 5.9 %fusion.57 = (bf16[3072]{0:T(1024)(128)(2,1)}, bf16[128,3072]{1,0:T(8,128)(2,1)S(1)}) fusion(f32[128,3072]{1,0:T(8,128)} %get-tuple-element.116, bf16[128,768]{1,0:T(8,128)(2,1)S(1)} %copy-done.17, bf16[1,3072,768]{2,1,0:T(8,128)(2,1)} %all-gather.27.cloned.1.call-done), kind=kOutput, calls=%fused_computation.109 | convolution fusion | flops 613807104 | bytes 7280640 | tf_op jit(solution)/shard_map/dot_general | solution.py:42
  190.0 2.3 multiply_reduce_fusion.1
  193.1 0.7 fusion.50
  193.8 0.7 copy-done.13
  194.4 1.5 convolution_convert_fusion.2
  196.2 2.1 fusion.35
  198.3 1.1 copy.49
  199.4 1.3 multiply_reduce_fusion
  202.0 3.0 convolution_convert_fusion.1
  205.1 1.0 copy-done.8
  206.1 3.7 convolution_convert_fusion
  209.8 1.1 copy-done.9
  211.0 1.0 copy.60
  211.9 4.3 %all-to-all-start = ((bf16[128,8,384]{2,0,1:T(8,128)(2,1)}), bf16[128,8,384]{2,0,1:T(8,128)(2,1)}, u32[]{:S(2)}, u32[]{:S(2)}) async-start(bf16[128,8,384]{2,0,1:T(8,128)(2,1)} %bitcast.133), calls=%async_computation.3 | async-start | bytes 1572864 | tf_op jit(solution)/shard_map/all_to_all | solution.py:253
  217.9 1.7 convert_reduce_fusion
  219.6 0.6 convert_bitcast_fusion
  220.4 0.6 fusion.53
  221.1 4.8 %multiply_reduce_fusion.2 = (bf16[768]{0:T(1024)(128)(2,1)}, f32[128]{0:T(128)}, bf16[768]{0:T(1024)(128)(2,1)}, f32[128,768]{1,0:T(8,128)}) fusion(f32[128,768]{1,0:T(8,128)S(1)} %copy-done, f32[128]{0:T(128)} %copy-done.31, f32[128]{0:T(128)S(1)} %copy-done.28, f32[768]{0:T(1024)S(1)} %convert_element_type.288, ...), kind=kOutput, calls=%fused_computation.57 | convolution fusion | flops 455539072 | bytes 4922880 | tf_op jit(solution)/shard_map/dot_general | solution.py:42
  225.9 35.2 %all-reduce.16 = (bf16[768]{0:T(1024)(128)(2,1)S(1)}, bf16[768]{0:T(1024)(128)(2,1)S(1)}, bf16[768]{0:T(1024)(128)(2,1)S(1)}, bf16[768]{0:T(1024)(128)(2,1)S(1)}...) all-reduce(bf16[768]{0:T(1024)(128)(2,1)} %copy-done.38, ...), channel_id=14, replica_groups=mesh['rep'=4,'shard'=8] {'shard'}, use_global_device_ids=true, to_apply=%add.7 | all-reduce | flops 9216 | bytes 36864
  261.2 2.8 fusion.24
  264.0 32.5 %reduce-scatter.4.cloned.1.call-done = bf16[96,2304]{1,0:T(8,128)(2,1)} async-done(((bf16[768,2304]{1,0:T(8,128)(2,1)}), bf16[96,2304]{1,0:T(8,128)(2,1)}) %reduce-scatter.4.cloned.1.call-update) | async-done | bytes 442384 | tf_op jit(solution)/shard_map/reduce_scatter | solution.py:78
  296.5 55.8 %reduce-scatter.8.cloned.1.call-done = bf16[96,3072]{1,0:T(8,128)(2,1)} async-done(((bf16[768,3072]{1,0:T(8,128)(2,1)}), bf16[96,3072]{1,0:T(8,128)(2,1)}) %reduce-scatter.8.cloned.1.call-update) | async-done | bytes 589840 | tf_op jit(solution)/shard_map/reduce_scatter | solution.py:99
  352.6 10.1 %all-reduce.18 = (bf16[1,96]{1,0:T(2,128)(2,1)S(1)}, bf16[1,96]{1,0:T(2,128)(2,1)S(1)}, bf16[1,96]{1,0:T(2,128)(2,1)S(1)}, bf16[1,96]{1,0:T(2,128)(2,1)S(1)}, bf...) all-reduce(bf16[1,96]{1,0:T(2,128)(2,1)S(1)} %dynamic-slice_bitcast, ...), channel_id=1, replica_groups=mesh['rep'=4,'shard'=8] {'rep'}, use_global_device_ids=true, to_apply=%region_13.14 | all-reduce | flops 1152 | bytes 4608 | tf_op jit(solution)/shard_map/psum | solution.py:107
  362.7 0.5 stack.79
  363.8 0.5 stack.85
  364.8 0.5 stack.91
  366.3 0.6 stack.99
  367.7 0.9 add_add_fusion.2
  368.6 3.9 fusion.29
  372.5 46.5 %all-reduce.22.cloned.1.call-done = (bf16[1,96,2304]{2,1,0:T(8,128)(2,1)}, bf16[1,96,768]{2,1,0:T(8,128)(2,1)}, bf16[1,96,3072]{2,1,0:T(8,128)(2,1)}, bf16[1,384,768]{2,1,0:T(8,128)(2,1)}) async-done(((bf16[1,96,2304]{2,1,0:T(8,128)(2,1)}, bf16[1,96,768]{2,1,0:T(8,128)(2,1)}, bf16[1,96,3072]{2,1,0:T(8,128)(2,1)}, bf16[1,384,768]{2,1,0:T(8,128)(2,1)}), (bf16[1,96,2304]{2,1,0:T(8,128)(2,1)}, ...) | async-done | bytes 1769488 | tf_op jit(solution)/shard_map/psum | solution.py:109
  419.0 2.1 stack.83
  421.1 1.6 stack.89
  422.7 1.1 stack.97
  423.8 1.1 stack.101
  (200 shorter events, 9.8 us)
Async XLA Ops:
  7.2 2.2 copy-start.21
  7.2 3.0 copy-start.15
  7.2 54.6 %all-gather.21.cloned.1.call-start = ((), (), s32[]{:S(2)}) async-start(), calls=%async_computation.8 | async-start | bytes 3981312 | tf_op jit(solution)/shard_map/all_gather | solution.py:56
  9.4 69.5 %all-gather.23.cloned.1.call-start = ((), (), s32[]{:S(2)}) async-start(), calls=%async_computation.9 | async-start | bytes 1327104 | tf_op jit(solution)/shard_map/all_gather | solution.py:59
  10.1 121.9 %all-gather.25.cloned.1.call-start = ((), (), s32[]{:S(2)}) async-start(), calls=%async_computation.10 | async-start | bytes 5308416 | tf_op jit(solution)/shard_map/all_gather | solution.py:63
  11.1 1.9 copy-start.50
  11.1 2.0 copy-start.51
  11.2 2.0 copy-start.52
  11.2 2.0 copy-start.53
  11.2 2.0 copy-start.42
  11.2 37.2 %copy-start = (f32[128,768]{1,0:T(8,128)S(1)}, f32[128,768]{1,0:T(8,128)}, u32[]{:S(2)}) copy-start(f32[128,768]{1,0:T(8,128)} %param.16) | copy-start | bytes 1179652
  11.2 172.9 %all-gather.27.cloned.1.call-start = ((), (), s32[]{:S(2)}) async-start(), calls=%async_computation.11 | async-start | bytes 5308416 | tf_op jit(solution)/shard_map/all_gather | solution.py:65
  12.1 36.7 %copy-start.41 = (s32[1,128]{1,0:T(1,128)S(1)}, s32[1,128]{1,0:T(1,128)}, u32[]{:S(2)}) copy-start(s32[1,128]{1,0:T(1,128)} %param.17) | copy-start | bytes 1540
  12.1 36.8 %copy-start.43 = (f32[1,384]{1,0:T(1,128)S(1)}, f32[1,384]{1,0:T(1,128)}, u32[]{:S(2)}) copy-start(f32[1,384]{1,0:T(1,128)} %param.29) | copy-start | bytes 4612
  12.2 205.7 %all-gather.19.cloned.1.call-start = ((), (), s32[]{:S(2)}) async-start(), calls=%async_computation.7 | async-start | bytes 1769472 | tf_op jit(solution)/shard_map/all_gather | solution.py:254
  12.9 251.1 %reduce-scatter.6.cloned.1.call-start = ((), (), s32[]{:S(2)}) async-start(), calls=%async_computation.5 | async-start | bytes 1327104 | tf_op jit(solution)/shard_map/reduce_scatter | solution.py:87
  48.4 13.4 %copy-start.22 = (f32[768]{0:T(1024)}, f32[768]{0:T(1024)S(1)}, u32[]{:S(2)}) copy-start(f32[768]{0:T(1024)S(1)} %convert_element_type.289) | copy-start | bytes 9220
  48.6 16.0 %copy-start.26 = (f32[128]{0:T(128)}, f32[128]{0:T(128)S(1)}, u32[]{:S(2)}) copy-start(f32[128]{0:T(128)S(1)} %broadcast_multiply_fusion.1) | copy-start | bytes 1540
  48.8 15.8 %copy-start.44 = (f32[128]{0:T(128)}, f32[128]{0:T(128)S(1)}, u32[]{:S(2)}) copy-start(f32[128]{0:T(128)S(1)} %multiply_reduce_fusion.6) | copy-start | bytes 1540
  48.8 15.8 %copy-start.31 = (f32[128]{0:T(128)}, f32[128]{0:T(128)S(1)}, u32[]{:S(2)}) copy-start(f32[128]{0:T(128)S(1)} %fusion.46) | copy-start | bytes 1540
  61.7 70.3 %copy-start.24 = (f32[768]{0:T(1024)}, f32[768]{0:T(1024)S(1)}, u32[]{:S(2)}) copy-start(f32[768]{0:T(1024)S(1)} %convert_element_type.292) | copy-start | bytes 9220
  65.7 71.4 %copy-start.11 = (bf16[12,64,128]{2,1,0:T(8,128)(2,1)}, bf16[12,64,128]{2,1,0:T(8,128)(2,1)S(1)}, u32[]{:S(2)}) copy-start(bf16[12,64,128]{2,1,0:T(8,128)(2,1)S(1)} %convolution_convert_fusion.5) | copy-start | bytes 589828
  80.6 111.7 %copy-start.29 = (f32[128]{0:T(128)}, f32[128]{0:T(128)S(1)}, u32[]{:S(2)}) copy-start(f32[128]{0:T(128)S(1)} %broadcast_multiply_fusion) | copy-start | bytes 1540
  80.8 111.5 %copy-start.34 = (f32[128]{0:T(128)}, f32[128]{0:T(128)S(1)}, u32[]{:S(2)}) copy-start(f32[128]{0:T(128)S(1)} %fusion.47) | copy-start | bytes 1540
  132.0 52.1 %copy-start.17 = (bf16[128,768]{1,0:T(8,128)(2,1)S(1)}, bf16[128,768]{1,0:T(8,128)(2,1)}, u32[]{:S(2)}) copy-start(bf16[128,768]{1,0:T(8,128)(2,1)} %convert_element_type.265) | copy-start | bytes 589828
  184.1 5.9 %copy-start.3 = (bf16[1,768,3072]{2,1,0:T(8,128)(2,1)S(1)}, bf16[1,768,3072]{2,1,0:T(8,128)(2,1)}, u32[]{:S(2)}) copy-start(bf16[1,768,3072]{2,1,0:T(8,128)(2,1)} %all-gather.25.cloned.1.call-done) | copy-start | bytes 14155780
  190.0 2.3 copy-start.7
  192.3 2.1 copy-start.12
  193.8 2.4 copy-start.2
  195.9 100.6 %reduce-scatter.4.cloned.1.call-start = ((), (), s32[]{:S(2)}) async-start(), calls=%async_computation.4 | async-start | bytes 3981312 | tf_op jit(solution)/shard_map/reduce_scatter | solution.py:78
  201.6 18.6 %copy-start.14 = (bf16[12,64,128]{2,1,0:T(8,128)(2,1)}, bf16[12,64,128]{2,1,0:T(8,128)(2,1)S(1)}, u32[]{:S(2)}) copy-start(bf16[12,64,128]{2,1,0:T(8,128)(2,1)S(1)} %fusion.38) | copy-start | bytes 589828
  205.0 147.3 %reduce-scatter.8.cloned.1.call-start = ((), (), s32[]{:S(2)}) async-start(), calls=%async_computation.6 | async-start | bytes 5308416 | tf_op jit(solution)/shard_map/reduce_scatter | solution.py:99
  210.9 6.7 %copy-start.54 = (f32[1,96]{1,0:T(1,128)S(1)}, f32[1,96]{1,0:T(1,128)}, u32[]{:S(2)}) copy-start(f32[1,96]{1,0:T(1,128)} %param.31) | copy-start | bytes 1156
  211.9 9.1 %copy-start.28 = (f32[128]{0:T(128)S(1)}, f32[128]{0:T(128)}, u32[]{:S(2)}) copy-start(f32[128]{0:T(128)} %copy-done.26) | copy-start | bytes 1540
  211.9 49.3 %all-to-all-start = ((bf16[128,8,384]{2,0,1:T(8,128)(2,1)}), bf16[128,8,384]{2,0,1:T(8,128)(2,1)}, u32[]{:S(2)}, u32[]{:S(2)}) async-start(bf16[128,8,384]{2,0,1:T(8,128)(2,1)} %bitcast.133), calls=%async_computation.3 | async-start | bytes 1572864 | tf_op jit(solution)/shard_map/all_to_all | solution.py:253
  216.3 202.7 %all-reduce.22.cloned.1.call-start = ((), (), s32[]{:S(2)}) async-start(), calls=%async_computation.12 | async-start | bytes 3538944 | tf_op jit(solution)/shard_map/psum | solution.py:109
  221.1 4.8 %copy-start.36 = (bf16[768]{0:T(1024)(128)(2,1)S(1)}, bf16[768]{0:T(1024)(128)(2,1)}, u32[]{:S(2)}) copy-start(bf16[768]{0:T(1024)(128)(2,1)} %get-tuple-element.56) | copy-start | bytes 4612
  221.1 4.8 %copy-start.37 = (bf16[768]{0:T(1024)(128)(2,1)S(1)}, bf16[768]{0:T(1024)(128)(2,1)}, u32[]{:S(2)}) copy-start(bf16[768]{0:T(1024)(128)(2,1)} %get-tuple-element.70) | copy-start | bytes 4612
  221.1 40.1 %copy-start.1 = (bf16[1024,768]{1,0:T(8,128)(2,1)S(1)}, bf16[1024,768]{1,0:T(8,128)(2,1)}, u32[]{:S(2)}) copy-start(bf16[1024,768]{1,0:T(8,128)(2,1)} %all-gather.19.cloned.1.call-done) | copy-start | bytes 4718596
  264.0 88.7 %copy-start.46 = (bf16[1,96]{1,0:T(2,128)(2,1)S(1)}, bf16[1,96]{1,0:T(2,128)(2,1)}, u32[]{:S(2)}) copy-start(bf16[1,96]{1,0:T(2,128)(2,1)} %convert_bitcast_fusion) | copy-start | bytes 580
  264.0 103.4 %copy-start.45 = (f32[128]{0:T(128)S(1)}, f32[128]{0:T(128)}, u32[]{:S(2)}) copy-start(f32[128]{0:T(128)} %copy-done.44) | copy-start | bytes 1540
  264.0 103.4 %copy-start.55 = (f32[128]{0:T(128)S(1)}, f32[128]{0:T(128)}, u32[]{:S(2)}) copy-start(f32[128]{0:T(128)} %get-tuple-element.69) | copy-start | bytes 1540
  264.0 103.5 %copy-start.20 = (f32[128,768]{1,0:T(8,128)S(1)}, f32[128,768]{1,0:T(8,128)}, u32[]{:S(2)}) copy-start(f32[128,768]{1,0:T(8,128)} %get-tuple-element.120) | copy-start | bytes 1179652
  264.0 103.5 %copy-start.33 = (f32[128]{0:T(128)S(1)}, f32[128]{0:T(128)}, u32[]{:S(2)}) copy-start(f32[128]{0:T(128)} %copy-done.31) | copy-start | bytes 1540
  264.0 103.7 %copy-start.40 = (f32[128]{0:T(128)S(1)}, f32[128]{0:T(128)}, u32[]{:S(2)}) copy-start(f32[128]{0:T(128)} %copy-done.39) | copy-start | bytes 1540
  352.3 16.3 %copy-start.10 = (bf16[128,3072]{1,0:T(8,128)(2,1)S(1)}, bf16[128,3072]{1,0:T(8,128)(2,1)}, u32[]{:S(2)}) copy-start(bf16[128,3072]{1,0:T(8,128)(2,1)} %get-tuple-element.115) | copy-start | bytes 2359300
  419.0 3.7 copy-start.19
  419.0 4.8 %copy-start.18 = (bf16[1,384,768]{2,1,0:T(8,128)(2,1)S(1)}, bf16[1,384,768]{2,1,0:T(8,128)(2,1)}, u32[]{:S(2)}) copy-start(bf16[1,384,768]{2,1,0:T(8,128)(2,1)} %get-tuple-element.100) | copy-start | bytes 1769476
  (18 other events, 22.9 us)
Sparse Core Ops, SparseCore 0:
  10.2 44.7 all-gather.20
  57.2 21.6 all-gather.22
  81.1 50.8 all-gather.24
  134.1 49.9 all-gather.26
  186.1 24.0 all-gather.18
  212.9 36.2 reduce-scatter.5
  251.5 44.9 reduce-scatter.3
  298.8 53.4 reduce-scatter.7
  356.3 62.6 all-reduce.21
where the time goes:
time: 432 us; the launch traced here: 431 us
  waiting for transfers between devices  246 us (57%)
  blocking collectives  90.6 us (21%)
  matrix products  42.4 us (10%)
  other arithmetic  20.8 us (5%)
  between operations  16.6 us (4%)
  local copies, waits for them, and re-layouts  9.89 us (2%)
  starting transfers between devices  4.9 us (1%)
    reduce_scatter x1, waiting for transfers between devices, reduce_nested_rest(): lax.psum_scatter(grads[9].astype(jnp.bfloat16), 'shard', scatter_dimensio...  55.8 us
    all_gather x1, waiting for transfers between devices, fetch_forward(): lax.all_gather(parts[9], 'shard', axis=0, tiled=True)  51.2 us
    all_gather x1, waiting for transfers between devices, fetch_forward(): lax.all_gather(parts[11], 'shard', axis=0, tiled=True)  47 us
    psum x1, waiting for transfers between devices, reduce_nested_rest(): lax.psum(owned[2].astype(jnp.bfloat16), 'rep').astype(jnp.float32)  46.5 us
    unnamed x1, blocking collectives  35.2 us
    all_gather x1, blocking collectives, fetch_forward(): lax.all_gather(parts[4], 'shard', axis=0, tiled=True)  32.5 us
    reduce_scatter x1, waiting for transfers between devices, reduce_nested_rest(): lax.psum_scatter(grads[2].astype(jnp.bfloat16), 'shard', scatter_dimensio...  32.5 us
    dot_general x4, matrix products, project_trans(): lax.dot_general(left, right, (((1,), (1,)), ((), ())), preferred_element_...  15.2 us
  transfers between devices with their start and end apart: 10, of which 6 were waited for; matrix products, arithmetic and copies ran while one was open for 14% of the time, Pallas kernels for 0%

commit v1 on v0

v1 whole, which is shorter than its diff:
```python
import jax
import jax.numpy as jnp
from jax import lax
from jax.experimental import pallas as pl
from jax.experimental.pallas import tpu as pltpu
from jax.sharding import PartitionSpec as P

HEADS = 12
HEAD = 64

EPS = 1e-05
GELU_C = 0.7978845608028654
NEG_FILL = -1e30
BF = jnp.bfloat16
F32 = jnp.float32


def mm(left, right):
    return jnp.dot(left, right, preferred_element_type=F32)


def mm_tn(left, right):
    return lax.dot_general(left, right, (((0,), (0,)), ((), ())), preferred_element_type=F32)


def mm_nt(left, right):
    return lax.dot_general(left, right, (((1,), (1,)), ((), ())), preferred_element_type=F32)


def norm_parts(rows):
    average = jnp.mean(rows, axis=-1, keepdims=True)
    centred = rows - average
    spread = jnp.mean(centred * centred, axis=-1, keepdims=True)
    scale = lax.rsqrt(spread + EPS)
    return centred * scale, scale


def norm_back(grad, unit, scale, gain):
    weighted = grad * gain
    return scale * (
        weighted
        - jnp.mean(weighted, axis=-1, keepdims=True)
        - unit * jnp.mean(weighted * unit, axis=-1, keepdims=True)
    )


def gelu_and_slope(f):
    t = jnp.tanh(GELU_C * (f + 0.044715 * f * f * f))
    value = 0.5 * f * (1.0 + t)
    slope = 0.5 * (1.0 + t) + 0.5 * f * (1.0 - t * t) * GELU_C * (1.0 + 3 * 0.044715 * f * f)
    return value, slope


def swap_by_index(blocks, index):
    blocks = list(blocks)
    bit = 1
    while bit < len(blocks):
        flag = (index & bit) > 0
        for low in range(len(blocks)):
            if low & bit == 0:
                first, second = blocks[low], blocks[low | bit]
                blocks[low] = jnp.where(flag, second, first)
                blocks[low | bit] = jnp.where(flag, first, second)
        bit *= 2
    return blocks


def group_size():
    size = lax.axis_size("rep")
    while HEADS % size:
        size //= 2
    return size


def to_rep(block, step):
    count = lax.axis_size("rep")
    return lax.ppermute(block, "rep", [(one, one ^ step) for one in range(count)])


def to_shard(block, step):
    count = lax.axis_size("shard")
    return lax.ppermute(block, "shard", [(one, one ^ step) for one in range(count)])


def to_side(block, level):
    reps, shards = lax.axis_size("rep"), lax.axis_size("shard")
    bits = group_size().bit_length() - 1
    pairs = []
    for one in range(reps):
        for place in range(shards):
            step = 1 << ((level + (place & 1)) % bits)
            pairs.append((one * shards + place, (one ^ step) * shards + place))
    return lax.ppermute(block, ("rep", "shard"), pairs)


def sides():
    return range(group_size().bit_length() - 1)


def gather_side(block):
    held = block[None]
    for level in sides():
        held = jnp.concatenate([held, to_side(held, level)], axis=0)
    return held


def reduce_side(low, high):
    total = low
    for level in reversed(sides()):
        if high is None:
            half = total.shape[0] // 2
            total, high = total[:half], total[half:].astype(BF)
        total = total + to_side(high, level).astype(F32)
        high = None
    return total[0]


def in_order(blocks, me):
    bits = group_size().bit_length() - 1
    core = lax.axis_index("shard") & 1
    if bits == 2:
        first, second = blocks[1], blocks[2]
        blocks = [blocks[0], jnp.where(core == 0, first, second),
                  jnp.where(core == 0, second, first), blocks[3]]
    return swap_by_index(blocks, me)


def from_order(blocks, me):
    bits = group_size().bit_length() - 1
    core = lax.axis_index("shard") & 1
    blocks = swap_by_index(blocks, me)
    if bits == 2:
        first, second = blocks[1], blocks[2]
        blocks = [blocks[0], jnp.where(core == 0, first, second),
                  jnp.where(core == 0, second, first), blocks[3]]
    return blocks


def exchange_side(blocks):
    held = jnp.stack(blocks)
    for level in sides():
        step = 1 << level
        pairs = held.reshape((-1, 2, step) + held.shape[1:])
        moved = to_side(pairs[:, 1], level)
        held = jnp.stack([pairs[:, 0], moved], axis=1).reshape(held.shape)
    return held


def after(block, *others):
    return lax.optimization_barrier((block,) + others)[0]


def place_kernel(at_ref, near_ref, far_ref, *out_refs):
    at = at_ref[0]
    for i in range(near_ref.shape[0]):
        for j, source in enumerate((near_ref, far_ref)):
            top = 0
            for out_ref in out_refs:
                rows, columns = out_ref.shape[1:]
                piece = source[i, top:top + rows, :columns]
                out_ref[at ^ (2 * i + j)] = piece.astype(out_ref.dtype)
                top += rows


def gather_links(block):
    count = lax.axis_size("shard") // 2
    return [block] + [to_shard(block, 2 * step) for step in range(1, count)]


def gather_pair(blocks, *parts):
    near = jnp.stack(blocks)
    far = to_shard(near, 1)
    place = lax.axis_index("shard").astype(jnp.int32).reshape(1)
    count = 2 * len(blocks)
    return pl.pallas_call(
        place_kernel,
        out_shape=[jax.ShapeDtypeStruct((count,) + shape, dtype) for shape, dtype in parts],
        in_specs=[pl.BlockSpec(memory_space=pltpu.SMEM), pl.BlockSpec(), pl.BlockSpec()],
    )(place, near, far)


def call(kernel, scalar, operands, outs):
    return pl.pallas_call(
        kernel,
        out_shape=[jax.ShapeDtypeStruct(shape, dtype) for shape, dtype in outs],
        in_specs=[pl.BlockSpec(memory_space=pltpu.SMEM)] + [pl.BlockSpec()] * len(operands),
    )(scalar, *operands)


def choose(index, pieces):
    out = pieces[0]
    for i in range(1, len(pieces)):
        out = jnp.where(index == i, pieces[i], out)
    return out


def pack_kernel(at_ref, w_ref, *refs):
    out_ref = refs[-1]
    rows = w_ref.shape[0]
    part = out_ref.shape[1] // 3
    ranks = w_ref.shape[1] // (3 * part)
    for j in range(3):
        first = j * ranks * part
        out_ref[0:rows, j * part:(j + 1) * part] = choose(
            at_ref[0], [w_ref[:, first + i * part:first + (i + 1) * part] for i in range(ranks)]
        ).astype(BF)
    lines = [ref[:, i:i + rows] for ref in refs[:-1] for i in range(0, ref.shape[1], rows)]
    out_ref[rows:rows + len(lines), 0:rows] = jnp.concatenate(lines, axis=0).astype(BF)


def pack_mlp_kernel(at_ref, up_ref, down_ref, out_ref):
    rows = up_ref.shape[0]
    hid = down_ref.shape[0]
    ranks = up_ref.shape[1] // (out_ref.shape[1] - down_ref.shape[1])
    part = hid // ranks
    for s in range(up_ref.shape[1] // hid):
        out_ref[:, s * part:(s + 1) * part] = choose(
            at_ref[0],
            [up_ref[:, s * hid + i * part:s * hid + (i + 1) * part] for i in range(ranks)]
        ).astype(BF)
    first = out_ref.shape[1] - down_ref.shape[1]
    out_ref[:, first:] = choose(
        at_ref[0], [down_ref[i * part:(i + 1) * part, :] for i in range(ranks)]).astype(BF)


def start_kernel(_, hidden_ref, cot_ref, docs_ref, out_ref):
    tokens, width = hidden_ref.shape
    out_ref[0:tokens] = norm_parts(hidden_ref[...])[0].astype(BF)
    out_ref[tokens:2 * tokens] = cot_ref[...].astype(BF)
    docs = docs_ref[...].astype(F32)
    line = jnp.concatenate([docs, jnp.zeros((1, width - tokens), F32)], axis=1)
    out_ref[2 * tokens:2 * tokens + 16] = jnp.broadcast_to(line, (16, width)).astype(BF)


def attend_kernel(_, all_ref, w_ref, gain_ref, shift_ref, bias_ref,
                  normed_ref, dm_ref, packed_ref, p_ref, out_ref):
    ranks, tokens, part = out_ref.shape
    heads = part // HEAD
    gain, shift = gain_ref[...], shift_ref[...]
    for g in range(ranks):
        span = slice(g * tokens, (g + 1) * tokens)
        normed_ref[span] = (all_ref[g, 0:tokens].astype(F32) * gain + shift).astype(BF)
        dm_ref[span] = all_ref[g, tokens:2 * tokens]
    packed_ref[...] = (mm(normed_ref[...], w_ref[...]) + bias_ref[...]).astype(BF)
    rows = lax.broadcasted_iota(jnp.int32, (tokens, tokens), 0)
    columns = lax.broadcasted_iota(jnp.int32, (tokens, tokens), 1)
    for g in range(ranks):
        span = slice(g * tokens, (g + 1) * tokens)
        line = all_ref[g, 2 * tokens:2 * tokens + 16, 0:tokens].astype(F32)[0:1]
        across = jnp.broadcast_to(line, (tokens, tokens))
        allowed = (rows >= columns) & (across == across.T)
        for h in range(heads):
            q = packed_ref[span, h * HEAD:(h + 1) * HEAD]
            k = packed_ref[span, part + h * HEAD:part + (h + 1) * HEAD]
            v = packed_ref[span, 2 * part + h * HEAD:2 * part + (h + 1) * HEAD]
            scores = jnp.where(allowed, mm_nt(q, k) * 0.125, NEG_FILL)
            powers = jnp.exp(scores - jnp.max(scores, axis=-1, keepdims=True))
            p = powers / jnp.sum(powers, axis=-1, keepdims=True)
            p_ref[g * heads + h] = p
            out_ref[g, :, h * HEAD:(h + 1) * HEAD] = mm(p.astype(BF), v).astype(BF)


def attend_back_kernel(at_ref, packed_ref, p_ref, do_ref, normed_ref, w_ref,
                       low_ref, high_ref, mine_ref, other_ref, sums_ref, grad_ref):
    ranks, tokens, part = do_ref.shape
    heads = part // HEAD
    for g in range(ranks):
        span = slice(g * tokens, (g + 1) * tokens)
        for h in range(heads):
            cq = slice(h * HEAD, (h + 1) * HEAD)
            ck = slice(part + h * HEAD, part + (h + 1) * HEAD)
            cv = slice(2 * part + h * HEAD, 2 * part + (h + 1) * HEAD)
            p = p_ref[g * heads + h]
            do = do_ref[g, :, cq]
            dp = mm_nt(do, packed_ref[span, cv])
            ds = (p * (dp - jnp.sum(dp * p, axis=-1, keepdims=True))).astype(BF)
            grad_ref[span, cv] = mm_tn(p.astype(BF), do).astype(BF)
            grad_ref[span, cq] = (mm(ds, packed_ref[span, ck]) * 0.125).astype(BF)
            grad_ref[span, ck] = (mm_tn(ds, packed_ref[span, cq]) * 0.125).astype(BF)
    grad = grad_ref[...]
    sums_ref[...] = jnp.sum(grad.astype(F32), axis=0, keepdims=True)
    split_rows(at_ref, mm_tn(normed_ref[...], grad), mine_ref, other_ref)
    half = ranks // 2
    for g in range(ranks):
        block = mm_nt(grad[g * tokens:(g + 1) * tokens], w_ref[...])
        if g < half:
            low_ref[g] = block
        else:
            high_ref[g - half] = block.astype(BF)


def split_rows(at_ref, whole, mine_ref, other_ref):
    rows = mine_ref.shape[1]
    even = at_ref[0] == 0
    for i in range(mine_ref.shape[0]):
        first = whole[2 * i * rows:(2 * i + 1) * rows]
        second = whole[(2 * i + 1) * rows:(2 * i + 2) * rows]
        mine_ref[i] = jnp.where(even, first, second)
        other_ref[i] = jnp.where(even, second, first).astype(BF)


def finish_kernel(at_ref, hidden_ref, grad_ref, middle_ref, gain_ref, bias_ref, hid_ref, rest_ref,
                  input_ref, mine_ref, other_ref):
    unit, scale = norm_parts(hidden_ref[...])
    grad = grad_ref[...]
    input_ref[...] = middle_ref[...] + norm_back(grad, unit, scale, gain_ref[...])
    width = grad.shape[1]
    part = bias_ref.shape[1] // 3
    ranks = width // part
    me, even = at_ref[1], at_ref[0] == 0

    def spread(first):
        piece = bias_ref[:, first:first + part]
        return jnp.concatenate(
            [jnp.where(me == i, piece, 0.0) for i in range(ranks)], axis=1)

    lines = [jnp.sum(grad * unit, axis=0, keepdims=True), jnp.sum(grad, axis=0, keepdims=True),
             spread(0), spread(2 * part), rest_ref[...]]
    lines = jnp.concatenate(lines, axis=0)
    hid = hid_ref[...]
    shards = 2 * mine_ref.shape[0]
    rows = width // shards
    per = hid.shape[1] // shards
    blocks = []
    for s in range(shards):
        own = jnp.concatenate(
            [jnp.where(me == i, hid[:, s * per:(s + 1) * per], 0.0) for i in range(ranks)], axis=1)
        own = [own[:, i:i + rows] for i in range(0, ranks * per, rows)]
        blocks.append(jnp.concatenate([lines[:, s * rows:(s + 1) * rows]] + own, axis=0))
    for i in range(mine_ref.shape[0]):
        mine_ref[i] = jnp.where(even, blocks[2 * i], blocks[2 * i + 1])
        other_ref[i] = jnp.where(even, blocks[2 * i + 1], blocks[2 * i]).astype(BF)


def split_shard(grad):
    shards = grad.shape[0]
    core = lax.axis_index("shard") & 1
    pairs = grad.reshape((shards // 2, 2) + grad.shape[1:])
    other = lax.dynamic_index_in_dim(pairs, core ^ 1, 1, keepdims=False)
    return lax.dynamic_index_in_dim(pairs, core, 1, keepdims=False), other.astype(BF)


def reduce_shard(mine, other):
    links = mine.shape[0]
    place = lax.axis_index("shard") >> 1
    mine = mine + to_shard(other, 1).astype(F32)
    total = lax.dynamic_index_in_dim(mine, place, 0, keepdims=False)
    mine = mine.astype(BF)
    for step in range(1, links):
        block = lax.dynamic_index_in_dim(mine, place ^ step, 0, keepdims=False)
        total = total + to_shard(block, 2 * step).astype(F32)
    step = group_size()
    while step < lax.axis_size("rep"):
        total = total + to_rep(total.astype(BF), step).astype(F32)
        step *= 2
    return total.astype(BF)


def split_plan(
    hidden, doc_ids, cotangent, pre_gain, pre_shift, qkv_weight, query_bias, value_bias,
    out_weight, out_bias, post_gain, post_shift, up_weight, up_bias, down_weight, down_bias,
):
    ranks = group_size()
    shards = lax.axis_size("shard")
    me = lax.axis_index("rep") & (ranks - 1)
    tokens, width = hidden.shape
    rows = qkv_weight.shape[1]
    part = width // ranks
    hid_rows = down_weight.shape[1]
    hid_part = hid_rows // ranks
    heads = HEADS // ranks

    core = lax.axis_index("shard") & 1
    at = jnp.stack([core, me]).astype(jnp.int32)
    mine = me.astype(jnp.int32).reshape(1)
    vectors = [pre_gain, pre_shift, query_bias, value_bias, out_bias, post_gain, post_shift,
               down_bias, up_bias]
    count = 8 + hid_rows // rows
    sent, = call(start_kernel, mine, (hidden, cotangent, doc_ids),
                 [((2 * tokens + 16, width), BF)])
    w_qkv, = call(pack_kernel, mine, [qkv_weight[0]] + vectors, [((rows + count, 3 * part), BF)])
    qkv_links = gather_links(w_qkv)
    every = gather_side(sent)
    w_qkv, vec = gather_pair(qkv_links, ((rows, 3 * part), BF), ((count, rows), F32))
    w_qkv = w_qkv.reshape(width, 3 * part)
    w_out = after(out_weight[0].astype(BF), *qkv_links)
    out_links = gather_links(w_out)
    w_out, = gather_pair(out_links, ((rows, width), BF))
    w_out = w_out.reshape(width, width)
    w_mlp, = call(pack_mlp_kernel, mine, (up_weight[0], down_weight[0]),
                  [((rows, shards * hid_part + width), BF)])
    mlp_links = gather_links(after(w_mlp, *out_links))
    w_mlp, = gather_pair(mlp_links, ((rows, shards * hid_part + width), BF))
    w_mlp = w_mlp.reshape(width, -1)
    w_up, w_down = w_mlp[:, :shards * hid_part], w_mlp[:, shards * hid_part:]

    lines = vec.transpose(1, 0, 2)
    p_gain, p_shift, q_bias, v_bias, o_bias, s_gain, s_shift, d_bias = [
        lines[i].reshape(1, width) for i in range(8)
    ]
    hid_bias = lines[8:].transpose(1, 0, 2).reshape(shards, ranks, hid_part)
    u_bias = lax.dynamic_index_in_dim(hid_bias, me, 1, keepdims=False).reshape(1, -1)

    def quarter(vector):
        return lax.dynamic_slice_in_dim(vector, me * part, part, 1)

    bias_row = jnp.concatenate([quarter(q_bias), jnp.zeros((1, part), F32), quarter(v_bias)], axis=1)
    whole = ranks * tokens
    normed_all, grad_down_all, packed, weights, mixed = call(
        attend_kernel, mine, (every, w_qkv, p_gain, p_shift, bias_row),
        [((whole, width), BF), ((whole, width), BF), ((whole, 3 * part), BF),
         ((ranks * heads, tokens, tokens), F32), ((ranks, tokens, part), BF)])
    mixed = exchange_side([mixed[i] for i in range(ranks)])
    mixed = jnp.concatenate(in_order([mixed[i] for i in range(ranks)], me), axis=1)
    middle = hidden + mm(mixed, w_out) + o_bias
    unit2, scale2 = norm_parts(middle)
    normed_two = (unit2 * s_gain + s_shift).astype(BF)
    normed_two_all = gather_side(normed_two).reshape(whole, width)
    pre_act = mm(normed_two_all, w_up) + u_bias
    activ, slope = gelu_and_slope(pre_act)
    activ = activ.astype(BF)

    half = ranks // 2
    grad_pre = (mm_nt(grad_down_all, w_down) * slope).astype(BF)
    sum_two = mm_nt(grad_pre, w_up).reshape(ranks, tokens, width)
    grad_two = reduce_side(sum_two[:half], sum_two[half:].astype(BF))
    g_s_gain = jnp.sum(grad_two * unit2, axis=0, keepdims=True)
    g_s_shift = jnp.sum(grad_two, axis=0, keepdims=True)
    grad_middle = cotangent + norm_back(grad_two, unit2, scale2, s_gain)
    grad_attn = grad_middle.astype(BF)
    grad_mixed = mm_nt(grad_attn, w_out).astype(BF)
    blocks = [grad_mixed[:, i * part:(i + 1) * part] for i in range(ranks)]
    grad_mixed = exchange_side(from_order(blocks, me))
    links = shards // 2
    low, high, qkv_mine, qkv_other, bias_sums, _ = call(
        attend_back_kernel, at, (packed, weights, grad_mixed, normed_all, w_qkv),
        [((half, tokens, width), F32), ((half, tokens, width), BF),
         ((links, rows, 3 * part), F32), ((links, rows, 3 * part), BF),
         ((1, 3 * part), F32), ((whole, 3 * part), BF)])
    grad_one = reduce_side(low, high)

    sum_out = mm(activ, w_down).reshape(ranks, tokens, width)
    hidden_out = reduce_side(sum_out[:half], sum_out[half:].astype(BF)) + (middle + d_bias)

    def by_shard(grad):
        return grad.reshape(shards, rows, -1)

    def every_rep(block):
        held = gather_side(block)
        return jnp.stack(in_order([held[i] for i in range(ranks)], me))

    g_mlp = reduce_shard(*split_shard(jnp.concatenate(
        [by_shard(mm_tn(normed_two_all, grad_pre)), by_shard(mm_tn(activ, grad_down_all))], axis=2)))
    g_mlp = every_rep(g_mlp)
    g_up = g_mlp[:, :, :shards * hid_part].astype(F32).reshape(ranks, rows, shards, hid_part)
    g_up = g_up.transpose(1, 2, 0, 3).reshape(1, rows, -1)
    g_down = g_mlp[:, :, shards * hid_part:].astype(F32).reshape(1, hid_rows, width)

    g_out = reduce_shard(*split_shard(by_shard(mm_tn(mixed, grad_attn))))
    g_out = jnp.sum(gather_side(g_out).astype(F32), axis=0)[None]

    g_qkv = every_rep(reduce_shard(qkv_mine, qkv_other)).astype(F32)
    g_qkv = g_qkv.reshape(ranks, rows, 3, part).transpose(1, 2, 0, 3).reshape(1, rows, -1)

    rest = jnp.concatenate([
        jnp.sum(grad_attn.astype(F32), axis=0, keepdims=True), g_s_gain, g_s_shift,
        jnp.sum(cotangent.astype(BF).astype(F32), axis=0, keepdims=True)], axis=0)
    hid_sums = jnp.sum(grad_pre.astype(F32), axis=0, keepdims=True)
    input_grad, sums_mine, sums_other = call(
        finish_kernel, at, (hidden, grad_one, grad_middle, p_gain, bias_sums, hid_sums, rest),
        [((tokens, width), F32), ((links, count, rows), F32), ((links, count, rows), BF)])
    sums = jnp.sum(gather_side(reduce_shard(sums_mine, sums_other)).astype(F32), axis=0)
    return (
        hidden_out, input_grad, sums[0:1], sums[1:2], g_qkv, sums[2:3], sums[3:4],
        g_out, sums[4:5], sums[5:6], sums[6:7], g_up, sums[8:].reshape(1, -1), g_down, sums[7:8],
    )


def solution(mesh):
    tokens = P(("rep", "shard"), None)
    vector = P(None, "shard")
    matrix = P(None, "shard", None)
    in_specs = (
        tokens, tokens, tokens, vector, vector, matrix, vector, vector, matrix, vector,
        vector, vector, matrix, vector, matrix, vector,
    )
    out_specs = (tokens, tokens) + in_specs[3:]
    return jax.shard_map(
        split_plan, mesh=mesh, in_specs=in_specs, out_specs=out_specs, check_vma=False
    )
```

time: 432 us -> 244 us (0.56)
  waiting for transfers between devices: 246 us -> 75.7 us
  blocking collectives: 90.6 us -> 0 us
  starting transfers between devices: 4.9 us -> 57.8 us
  Pallas kernels: 0 us -> 33.8 us
  matrix products: 42.4 us -> 13.6 us
  local copies, waits for them, and re-layouts: 9.89 us -> 29.4 us
  between operations: 16.6 us -> 1.52 us
  other arithmetic: 20.8 us -> 30.7 us
    all_gather x5 -> x0, waiting for transfers between devices: 111 us -> none  [the longest x1 51.2 us: fetch_forward(): lax.all_gather(parts[9], 'shard', axis=0, tiled=True)]
    reduce_scatter x3 -> x0, waiting for transfers between devices: 88.3 us -> none  [the longest x1 55.8 us: reduce_nested_rest(): lax.psum_scatter(grads[9].astype(jnp.bfloat16), 'shard', scatter_dimensio...]
    ppermute x0 -> x50, waiting for transfers between devices: none -> 75.7 us  [the longest x28 41.4 us: to_shard(): lax.ppermute(block, 'shard', [(one, one ^ step) for one in range(count)])]
    ppermute x0 -> x50, starting transfers between devices: none -> 57.8 us  [the longest x28 34.8 us: to_shard(): lax.ppermute(block, 'shard', [(one, one ^ step) for one in range(count)])]
    psum x1 -> x0, waiting for transfers between devices: 46.5 us -> none  [reduce_nested_rest(): lax.psum(owned[2].astype(jnp.bfloat16), 'rep').astype(jnp.float32)]
    all_gather x2 -> x0, blocking collectives: 45.3 us -> none  [the longest x1 32.5 us: fetch_forward(): lax.all_gather(parts[4], 'shard', axis=0, tiled=True)]
    unnamed x1 -> x0, blocking collectives: 35.2 us -> none
    pallas_call x0 -> x9, Pallas kernels: none -> 33.8 us  [the longest x6 26 us: call(): pl.pallas_call(kernel, out_shape=[jax.ShapeDtypeStruct(shape, dtype) for...]
  transfers between devices with their start and end apart: 10 -> 50, of which waited for: 6 -> 21; matrix products, arithmetic and copies ran while one was open for 14% -> 22% of each run, Pallas kernels for 0% -> 13%
where the time goes in v1:
time: 244 us; the launch traced here: 243 us
  waiting for transfers between devices  75.7 us (31%)
  starting transfers between devices  57.8 us (24%)
  Pallas kernels  33.8 us (14%)
  other arithmetic  30.7 us (13%)
  local copies, waits for them, and re-layouts  29.4 us (12%)
  matrix products  13.6 us (6%)
    ppermute x28, waiting for transfers between devices, to_shard(): lax.ppermute(block, 'shard', [(one, one ^ step) for one in range(count)])  41.4 us
    ppermute x28, starting transfers between devices, to_shard(): lax.ppermute(block, 'shard', [(one, one ^ step) for one in range(count)])  34.8 us
    ppermute x22, waiting for transfers between devices, to_side(): return lax.ppermute(block, ('rep', 'shard'), pairs)  34.3 us
    pallas_call x6, Pallas kernels, call(): pl.pallas_call(kernel, out_shape=[jax.ShapeDtypeStruct(shape, dtype) for...  26 us
    ppermute x22, starting transfers between devices, to_side(): return lax.ppermute(block, ('rep', 'shard'), pairs)  23 us
    pallas_call x3, Pallas kernels, gather_pair(): pl.pallas_call(place_kernel, out_shape=[jax.ShapeDtypeStruct((count,) + s...  7.78 us
    dot_general x3, matrix products, mm_tn(): lax.dot_general(left, right, (((0,), (0,)), ((), ())), preferred_element_...  6.47 us
    convert_element_type x4, other arithmetic, reduce_shard(): mine = mine.astype(BF)  5.78 us
  transfers between devices with their start and end apart: 50, of which 21 were waited for; matrix products, arithmetic and copies ran while one was open for 22% of the time, Pallas kernels for 13%

profile of v1, /device:TPU:0, one launch (start us, length us, event | category | flops | bytes accessed | tf_op | source)
XLA Modules:
  0.0 242.6 jit_solution(7145103189466957401)
XLA Ops:
  0.7 2.1 shard_map.271
  2.7 3.0 %collective-permute-start = (bf16[1,272,768]{2,1,0:T(8,128)(2,1)}, bf16[1,272,768]{2,1,0:T(8,128)(2,1)S(1)}, u32[]{:S(2)}, u32[]{:S(2)}) collective-permute-start(bf16[1,272,768]{2,1,0:T(8,128)(2,1)} %bitcast.260), channel_id=1, source_target_pairs={{0,8},{1,17},{2,10},{3,19},{4,12},{5,21},{6,14},{7,23},{8,0},{9,25... | collective-permute-start | bytes 1253384 | tf_op jit(solution)/shard_map/ppermute | solution.py:93
  5.7 2.3 shard_map.272
  8.0 3.6 %collective-permute-start.4 = (bf16[108,576]{1,0:T(8,128)(2,1)}, bf16[108,576]{1,0:T(8,128)(2,1)S(1)}, u32[]{:S(2)}, u32[]{:S(2)}) collective-permute-start(bf16[108,576]{1,0:T(8,128)(2,1)} %shard_map.272), channel_id=1, source_target_pairs={{0,6},{1,7},{2,4},{3,5},{4,2},{5,3},{6,0},{7,1},{8,14},{9,15},{10,... | collective-permute-start | bytes 373256 | tf_op jit(solution)/shard_map/ppermute | solution.py:82
  12.4 4.3 %collective-permute-done.4 = bf16[108,576]{1,0:T(8,128)(2,1)S(1)} collective-permute-done((bf16[108,576]{1,0:T(8,128)(2,1)}, bf16[108,576]{1,0:T(8,128)(2,1)S(1)}, u32[]{:S(2)}, u32[]{:S(2)}) %collective-permute-start.4) | collective-permute-done | bytes 124448 | tf_op jit(solution)/shard_map/ppermute | solution.py:82
  16.7 7.0 %collective-permute-done.3 = bf16[108,576]{1,0:T(8,128)(2,1)S(1)} collective-permute-done((bf16[108,576]{1,0:T(8,128)(2,1)}, bf16[108,576]{1,0:T(8,128)(2,1)S(1)}, u32[]{:S(2)}, u32[]{:S(2)}) %collective-permute-start.3) | collective-permute-done | bytes 124448 | tf_op jit(solution)/shard_map/ppermute | solution.py:82
  26.5 2.5 %collective-permute-start.10 = (bf16[96,768]{1,0:T(8,128)(2,1)S(1)}, bf16[96,768]{1,0:T(8,128)(2,1)S(1)}, u32[]{:S(2)}, u32[]{:S(2)}) collective-permute-start(bf16[96,768]{1,0:T(8,128)(2,1)S(1)} %convert_bitcast_fusion.1), channel_id=1, source_target_pairs={{0,6},{1,7},{2,4},{3,5},{4,2},{5,3},{6,0},{7,1},{8,14},{9,15},{10,... | collective-permute-start | bytes 442376 | tf_op jit(solution)/shard_map/ppermute | solution.py:82
  29.1 1.9 collective-permute-start.8
  31.1 3.3 %shard_map.276 = bf16[96,1536]{1,0:T(8,128)(2,1)} custom-call(s32[1]{0:T(128)} %bitcast._.at_ref, f32[96,3072]{1,0:T(8,128)} %bitcast.278, f32[384,768]{1,0:T(8,128)} %bitcast.279), custom_call_target="tpu_custom_call" | custom-call | tf_op jit(solution)/shard_map/pallas_call | solution.py:183
  35.1 6.7 %collective-permute-done.9 = bf16[96,768]{1,0:T(8,128)(2,1)S(1)} collective-permute-done((bf16[96,768]{1,0:T(8,128)(2,1)S(1)}, bf16[96,768]{1,0:T(8,128)(2,1)S(1)}, u32[]{:S(2)}, u32[]{:S(2)}) %collective-permute-start.9) | collective-permute-done | bytes 147488 | tf_op jit(solution)/shard_map/ppermute | solution.py:82
  42.4 2.2 collective-permute-start.16
  44.6 2.2 collective-permute-start.14
  47.7 2.3 shard_map.273
  54.8 7.6 %shard_map.274 = (bf16[512,768]{1,0:T(8,128)(2,1)}, bf16[512,768]{1,0:T(8,128)(2,1)}, bf16[512,576]{1,0:T(8,128)(2,1)}, f32[12,128,128]{2,1,0:T(8,128)}, bf16[4,128,192]{2,1,0:T(8,128)(2,1)}) custom-call(s32[1]{0:T(128)} %bitcast._.at_ref, bf16[4,272,768]{2,1,0:T(8,128)(2,1)} %pad_maximum_fusion.all_ref, bf16[768,576]{1,0:T(8,128)(2,1)} %bitcast.258, ...), custom_call_target="tpu_custom_call" | custom-call | tf_op jit(solution)/shard_map/pallas_call | solution.py:183
  65.6 2.8 %collective-permute-done.6 = bf16[2,1,128,192]{3,2,0,1:T(8,128)(2,1)S(1)} collective-permute-done((bf16[2,1,128,192]{3,2,0,1:T(8,128)(2,1)S(1)}, bf16[2,1,128,192]{3,2,0,1:T(8,128)(2,1)S(1)}, u32[]{:S(2)}, u32[]{:S(2)}) %collective-permute-start.6) | collective-permute-done | bytes 98336 | tf_op jit(solution)/shard_map/ppermute | solution.py:93
  72.6 2.3 shard_map.275
  78.4 5.0 %collective-permute-done.12 = bf16[1,128,768]{2,1,0:T(8,128)(2,1)S(1)} collective-permute-done((bf16[1,128,768]{2,1,0:T(8,128)(2,1)S(1)}, bf16[1,128,768]{2,1,0:T(8,128)(2,1)S(1)}, u32[]{:S(2)}, u32[]{:S(2)}) %collective-permute-start.12) | collective-permute-done | bytes 196640 | tf_op jit(solution)/shard_map/ppermute | solution.py:93
  87.3 3.2 %shard_map.277 = bf16[8,96,1536]{2,1,0:T(8,128)(2,1)} custom-call(s32[1]{0:T(128)} %bitcast.2.at_ref, bf16[4,96,1536]{2,1,0:T(8,128)(2,1)} %copy-done.10, bf16[4,96,1536]{2,1,0:T(8,128)(2,1)} %collective-permute-done.17.far_ref), custom_call_target="tpu_custom_call" | custom-call | tf_op jit(solution)/shard_map/pallas_call | solution.py:175
  91.5 2.2 convolution_add_fusion
  94.8 2.1 convert_reduce_fusion
  99.6 2.3 fusion.58
  105.1 2.1 fusion.20
  113.2 2.0 collective-permute-done.21
  115.5 2.7 %collective-permute-done.19 = bf16[1,128,768]{2,1,0:T(8,128)(2,1)S(1)} collective-permute-done((bf16[1,128,768]{2,1,0:T(8,128)(2,1)S(1)}, bf16[1,128,768]{2,1,0:T(8,128)(2,1)S(1)}, u32[]{:S(2)}, u32[]{:S(2)}) %collective-permute-start.19) | collective-permute-done | bytes 196640 | tf_op jit(solution)/shard_map/ppermute | solution.py:93
  118.2 1.6 convert_reduce_fusion.3
  123.2 2.6 %collective-permute-done.22 = bf16[2,1,128,192]{3,2,0,1:T(8,128)(2,1)S(1)} collective-permute-done((bf16[2,1,128,192]{3,2,0,1:T(8,128)(2,1)S(1)}, bf16[2,1,128,192]{3,2,0,1:T(8,128)(2,1)S(1)}, u32[]{:S(2)}, u32[]{:S(2)}) %collective-permute-start.22) | collective-permute-done | bytes 98336 | tf_op jit(solution)/shard_map/ppermute | solution.py:93
  126.6 2.0 fusion.52
  128.6 2.3 collective-permute-done.23
  131.6 8.3 %shard_map.278 = (f32[2,128,768]{2,1,0:T(8,128)}, bf16[2,128,768]{2,1,0:T(8,128)(2,1)}, f32[4,96,576]{2,1,0:T(8,128)}, bf16[4,96,576]{2,1,0:T(8,128)(2,1)}, f32[1,576]{1,0:T(1,128)}, /*index=5*/bf16[512,576]{1,0:T(8,128)(2,1)}) custom-call(s32[2]{0:T(128)} %pad_add_fusion.at_ref, bf16[512,576]{1,0:T(8,128)(2,1)} %get-tuple-element.37.packed_ref, ...), custom_call_target="tpu_custom_call" | custom-call | tf_op jit(solution)/shard_map/pallas_call | solution.py:183
  140.6 2.1 fusion.22
  144.6 3.4 %collective-permute-done.24 = bf16[2,128,768]{2,1,0:T(8,128)(2,1)} collective-permute-done((bf16[2,128,768]{2,1,0:T(8,128)(2,1)}, bf16[2,128,768]{2,1,0:T(8,128)(2,1)}, u32[]{:S(2)}, u32[]{:S(2)}) %collective-permute-start.24) | collective-permute-done | bytes 393248 | tf_op jit(solution)/shard_map/ppermute | solution.py:93
  152.1 2.1 collective-permute-start.41
  154.2 3.1 %fusion.59 = (bf16[4,96,1536]{2,1,0:T(8,128)(2,1)S(1)}, f32[4,96,1536]{2,1,0:T(8,128)}) fusion(bf16[4,96,1536]{2,1,0:T(8,128)(2,1)} %collective-permute-done.44, s32[]{:T(128)S(6)} %select_n.335, f32[4,2,96,768]{3,2,1,0:T(8,128)S(1)} %bitcast.252, f32[4,2,96,768]{3,2,1,0:T(8,128)S(1)} %fusion.20), kind=kLoop, calls=%fused_computation.198 | loop fusion | flops 2359296 | bytes 9437188 | tf_op jit(solution)/shard_map/convert_element_type | solution.py:348
  158.9 2.5 %shard_map.279 = (f32[128,768]{1,0:T(8,128)}, f32[4,12,96]{2,1,0:T(8,128)}, bf16[4,12,96]{2,1,0:T(8,128)(2,1)}) custom-call(s32[2]{0:T(128)} %pad_add_fusion.at_ref, f32[128,768]{1,0:T(8,128)} %hidden_ref.3, f32[128,768]{1,0:T(8,128)} %fusion.26.grad_ref, f32[128,768]{1,0:T(8,128)} %copy-done.6, f32[1,768]{1,0:T(1,128)} %reshape_squeeze.16.gain_ref, ...), custom_call_target="tpu_custom_call" | custom-call | tf_op jit(solution)/shard_map/pallas_call | solution.py:183
  162.9 1.8 collective-permute-start.29
  164.7 2.0 collective-permute-start.28
  169.2 2.1 collective-permute-start.47
  173.7 2.1 collective-permute-start.35
  178.4 17.7 %collective-permute-done.35 = bf16[96,576]{1,0:T(8,128)(2,1)S(1)} collective-permute-done((bf16[96,576]{1,0:T(8,128)(2,1)S(1)}, bf16[96,576]{1,0:T(8,128)(2,1)S(1)}, u32[]{:S(2)}, u32[]{:S(2)}) %collective-permute-start.35) | collective-permute-done | bytes 110624 | tf_op jit(solution)/shard_map/ppermute | solution.py:82
  196.1 7.3 %collective-permute-start.34 = (bf16[96,576]{1,0:T(8,128)(2,1)S(1)}, bf16[96,576]{1,0:T(8,128)(2,1)S(1)}, u32[]{:S(2)}, u32[]{:S(2)}) collective-permute-start(bf16[96,576]{1,0:T(8,128)(2,1)S(1)} %get-tuple-element.101), channel_id=1, source_target_pairs={{0,4},{1,5},{2,6},{3,7},{4,0},{5,1},{6,2},{7,3},{8,12},{9,13},{10,... | collective-permute-start | bytes 331784 | tf_op jit(solution)/shard_map/ppermute | solution.py:82
  203.4 3.7 %collective-permute-done.34 = bf16[96,576]{1,0:T(8,128)(2,1)S(1)} collective-permute-done((bf16[96,576]{1,0:T(8,128)(2,1)S(1)}, bf16[96,576]{1,0:T(8,128)(2,1)S(1)}, u32[]{:S(2)}, u32[]{:S(2)}) %collective-permute-start.34) | collective-permute-done | bytes 110624 | tf_op jit(solution)/shard_map/ppermute | solution.py:82
  209.6 2.8 %collective-permute-done.31 = bf16[2,12,96]{2,1,0:T(8,128)(2,1)S(1)} collective-permute-done((bf16[2,12,96]{2,1,0:T(8,128)(2,1)S(1)}, bf16[2,12,96]{2,1,0:T(8,128)(2,1)S(1)}, u32[]{:S(2)}, u32[]{:S(2)}) %collective-permute-start.31) | collective-permute-done | bytes 4640 | tf_op jit(solution)/shard_map/ppermute | solution.py:93
  216.9 1.7 collective-permute-done.36
  221.5 3.4 %collective-permute-done.48 = bf16[1,96,1536]{2,1,0:T(8,128)(2,1)S(1)} collective-permute-done((bf16[1,96,1536]{2,1,0:T(8,128)(2,1)S(1)}, bf16[1,96,1536]{2,1,0:T(8,128)(2,1)S(1)}, u32[]{:S(2)}, u32[]{:S(2)}) %collective-permute-start.48) | collective-permute-done | bytes 294944 | tf_op jit(solution)/shard_map/ppermute | solution.py:93
  228.7 1.7 reshape.200
  230.4 1.8 convert_reduce_fusion.1
  232.2 3.7 %collective-permute-done.49 = bf16[2,96,1536]{2,1,0:T(8,128)(2,1)S(1)} collective-permute-done((bf16[2,96,1536]{2,1,0:T(8,128)(2,1)}, bf16[2,96,1536]{2,1,0:T(8,128)(2,1)S(1)}, u32[]{:S(2)}, u32[]{:S(2)}) %collective-permute-start.49) | collective-permute-done | bytes 589856 | tf_op jit(solution)/shard_map/ppermute | solution.py:93
  238.9 2.6 %reshape.202 = f32[1,96,3072]{2,1,0:T(8,128)} reshape(f32[96,8,4,96]{3,2,1,0:T(4,128)S(1)} %copy.60) | data formatting | bytes 2359296 | tf_op jit(solution)/shard_map/reshape | solution.py:456
  (282 shorter events, 79.1 us)
Async XLA Ops:
  2.7 23.1 %collective-permute-start = (bf16[1,272,768]{2,1,0:T(8,128)(2,1)}, bf16[1,272,768]{2,1,0:T(8,128)(2,1)S(1)}, u32[]{:S(2)}, u32[]{:S(2)}) collective-permute-start(bf16[1,272,768]{2,1,0:T(8,128)(2,1)} %bitcast.260), channel_id=1, source_target_pairs={{0,8},{1,17},{2,10},{3,19},{4,12},{5,21},{6,14},{7,23},{8,0},{9,25... | collective-permute-start | bytes 1253384 | tf_op jit(solution)/shard_map/ppermute | solution.py:93
  8.0 8.7 %collective-permute-start.4 = (bf16[108,576]{1,0:T(8,128)(2,1)}, bf16[108,576]{1,0:T(8,128)(2,1)S(1)}, u32[]{:S(2)}, u32[]{:S(2)}) collective-permute-start(bf16[108,576]{1,0:T(8,128)(2,1)} %shard_map.272), channel_id=1, source_target_pairs={{0,6},{1,7},{2,4},{3,5},{4,2},{5,3},{6,0},{7,1},{8,14},{9,15},{10,... | collective-permute-start | bytes 373256 | tf_op jit(solution)/shard_map/ppermute | solution.py:82
  11.6 12.1 %collective-permute-start.3 = (bf16[108,576]{1,0:T(8,128)(2,1)}, bf16[108,576]{1,0:T(8,128)(2,1)S(1)}, u32[]{:S(2)}, u32[]{:S(2)}) collective-permute-start(bf16[108,576]{1,0:T(8,128)(2,1)} %shard_map.272), channel_id=1, source_target_pairs={{0,4},{1,5},{2,6},{3,7},{4,0},{5,1},{6,2},{7,3},{8,12},{9,13},{10,... | collective-permute-start | bytes 373256 | tf_op jit(solution)/shard_map/ppermute | solution.py:82
  11.7 12.1 %collective-permute-start.2 = (bf16[108,576]{1,0:T(8,128)(2,1)}, bf16[108,576]{1,0:T(8,128)(2,1)S(1)}, u32[]{:S(2)}, u32[]{:S(2)}) collective-permute-start(bf16[108,576]{1,0:T(8,128)(2,1)} %shard_map.272), channel_id=1, source_target_pairs={{0,2},{1,3},{2,0},{3,1},{4,6},{5,7},{6,4},{7,5},{8,10},{9,11},{10,... | collective-permute-start | bytes 373256 | tf_op jit(solution)/shard_map/ppermute | solution.py:82
  25.8 21.0 %collective-permute-start.5 = (bf16[4,108,576]{2,0,1:T(4,128)(2,1)}, bf16[4,108,576]{2,0,1:T(4,128)(2,1)S(1)}, u32[]{:S(2)}, u32[]{:S(2)}) collective-permute-start(bf16[4,108,576]{2,0,1:T(4,128)(2,1)} %copy.49), channel_id=1, source_target_pairs={{0,1},{1,0},{2,3},{3,2},{4,5},{5,4},{6,7},{7,6},{8,9},{9,8},{10,11... | collective-permute-start | bytes 1493000 | tf_op jit(solution)/shard_map/ppermute | solution.py:82
  25.9 27.5 %collective-permute-start.1 = (bf16[2,272,768]{2,1,0:T(8,128)(2,1)S(1)}, bf16[2,272,768]{2,1,0:T(8,128)(2,1)S(1)}, u32[]{:S(2)}, u32[]{:S(2)}) collective-permute-start(bf16[2,272,768]{2,1,0:T(8,128)(2,1)S(1)} %pad_maximum_fusion.3), channel_id=1, source_target_pairs={{0,16},{1,9},{2,18},{3,11},{4,20},{5,13},{6,22},{7,15},{8,24},{9,1... | collective-permute-start | bytes 2506760 | tf_op jit(solution)/shard_map/ppermute | solution.py:93
  26.5 8.6 %collective-permute-start.10 = (bf16[96,768]{1,0:T(8,128)(2,1)S(1)}, bf16[96,768]{1,0:T(8,128)(2,1)S(1)}, u32[]{:S(2)}, u32[]{:S(2)}) collective-permute-start(bf16[96,768]{1,0:T(8,128)(2,1)S(1)} %convert_bitcast_fusion.1), channel_id=1, source_target_pairs={{0,6},{1,7},{2,4},{3,5},{4,2},{5,3},{6,0},{7,1},{8,14},{9,15},{10,... | collective-permute-start | bytes 442376 | tf_op jit(solution)/shard_map/ppermute | solution.py:82
  29.1 12.7 %collective-permute-start.9 = (bf16[96,768]{1,0:T(8,128)(2,1)S(1)}, bf16[96,768]{1,0:T(8,128)(2,1)S(1)}, u32[]{:S(2)}, u32[]{:S(2)}) collective-permute-start(bf16[96,768]{1,0:T(8,128)(2,1)S(1)} %convert_bitcast_fusion.1), channel_id=1, source_target_pairs={{0,4},{1,5},{2,6},{3,7},{4,0},{5,1},{6,2},{7,3},{8,12},{9,13},{10,... | collective-permute-start | bytes 442376 | tf_op jit(solution)/shard_map/ppermute | solution.py:82
  29.1 13.4 %collective-permute-start.8 = (bf16[96,768]{1,0:T(8,128)(2,1)S(1)}, bf16[96,768]{1,0:T(8,128)(2,1)}, u32[]{:S(2)}, u32[]{:S(2)}) collective-permute-start(bf16[96,768]{1,0:T(8,128)(2,1)S(1)} %convert_bitcast_fusion.1), channel_id=1, source_target_pairs={{0,2},{1,3},{2,0},{3,1},{4,6},{5,7},{6,4},{7,5},{8,10},{9,11},{10,... | collective-permute-start | bytes 442376 | tf_op jit(solution)/shard_map/ppermute | solution.py:82
  42.4 27.8 %collective-permute-start.16 = (bf16[96,1536]{1,0:T(8,128)(2,1)}, bf16[96,1536]{1,0:T(8,128)(2,1)S(1)}, u32[]{:S(2)}, u32[]{:S(2)}) collective-permute-start(bf16[96,1536]{1,0:T(8,128)(2,1)} %shard_map.276), channel_id=1, source_target_pairs={{0,6},{1,7},{2,4},{3,5},{4,2},{5,3},{6,0},{7,1},{8,14},{9,15},{10,... | collective-permute-start | bytes 884744 | tf_op jit(solution)/shard_map/ppermute | solution.py:82
  44.6 25.6 %collective-permute-start.15 = (bf16[96,1536]{1,0:T(8,128)(2,1)}, bf16[96,1536]{1,0:T(8,128)(2,1)}, u32[]{:S(2)}, u32[]{:S(2)}) collective-permute-start(bf16[96,1536]{1,0:T(8,128)(2,1)} %shard_map.276), channel_id=1, source_target_pairs={{0,4},{1,5},{2,6},{3,7},{4,0},{5,1},{6,2},{7,3},{8,12},{9,13},{10,... | collective-permute-start | bytes 884744 | tf_op jit(solution)/shard_map/ppermute | solution.py:82
  44.6 25.6 %collective-permute-start.14 = (bf16[96,1536]{1,0:T(8,128)(2,1)}, bf16[96,1536]{1,0:T(8,128)(2,1)}, u32[]{:S(2)}, u32[]{:S(2)}) collective-permute-start(bf16[96,1536]{1,0:T(8,128)(2,1)} %shard_map.276), channel_id=1, source_target_pairs={{0,2},{1,3},{2,0},{3,1},{4,6},{5,7},{6,4},{7,5},{8,10},{9,11},{10,... | collective-permute-start | bytes 884744 | tf_op jit(solution)/shard_map/ppermute | solution.py:82
  63.4 5.0 %collective-permute-start.6 = (bf16[2,1,128,192]{3,2,0,1:T(8,128)(2,1)S(1)}, bf16[2,1,128,192]{3,2,0,1:T(8,128)(2,1)S(1)}, u32[]{:S(2)}, u32[]{:S(2)}) collective-permute-start(bf16[2,1,128,192]{3,2,0,1:T(8,128)(2,1)S(1)} %get-tuple-element.114), channel_id=1, source_target_pairs={{0,8},{1,17},{2,10},{3,19},{4,12},{5,21},{6,14},{7,23},{8,0},{9,25... | collective-permute-start | bytes 294920 | tf_op jit(solution)/shard_map/ppermute | solution.py:93
  65.5 6.3 %collective-permute-start.11 = (bf16[4,96,768]{2,1,0:T(8,128)(2,1)S(1)}, bf16[4,96,768]{2,1,0:T(8,128)(2,1)S(1)}, u32[]{:S(2)}, u32[]{:S(2)}) collective-permute-start(bf16[4,96,768]{2,1,0:T(8,128)(2,1)S(1)} %pad_maximum_fusion.5.near_ref), channel_id=1, source_target_pairs={{0,1},{1,0},{2,3},{3,2},{4,5},{5,4},{6,7},{7,6},{8,9},{9,8},{10,11... | collective-permute-start | bytes 1769480 | tf_op jit(solution)/shard_map/ppermute | solution.py:82
  69.2 5.7 %collective-permute-start.7 = (bf16[1,2,128,192]{3,2,1,0:T(8,128)(2,1)}, bf16[1,2,128,192]{3,2,1,0:T(8,128)(2,1)}, u32[]{:S(2)}, u32[]{:S(2)}) collective-permute-start(bf16[1,2,128,192]{3,2,1,0:T(8,128)(2,1)} %get-tuple-element.112), channel_id=1, source_target_pairs={{0,16},{1,9},{2,18},{3,11},{4,20},{5,13},{6,22},{7,15},{8,24},{9,1... | collective-permute-start | bytes 294920 | tf_op jit(solution)/shard_map/ppermute | solution.py:93
  71.5 15.8 %collective-permute-start.17 = (bf16[4,96,1536]{2,1,0:T(8,128)(2,1)S(1)}, bf16[4,96,1536]{2,1,0:T(8,128)(2,1)}, u32[]{:S(2)}, u32[]{:S(2)}) collective-permute-start(bf16[4,96,1536]{2,1,0:T(8,128)(2,1)S(1)} %pad_maximum_fusion.1.near_ref), channel_id=1, source_target_pairs={{0,1},{1,0},{2,3},{3,2},{4,5},{5,4},{6,7},{7,6},{8,9},{9,8},{10,11... | collective-permute-start | bytes 3538952 | tf_op jit(solution)/shard_map/ppermute | solution.py:82
  77.7 5.7 %collective-permute-start.12 = (bf16[1,128,768]{2,1,0:T(8,128)(2,1)S(1)}, bf16[1,128,768]{2,1,0:T(8,128)(2,1)S(1)}, u32[]{:S(2)}, u32[]{:S(2)}) collective-permute-start(bf16[1,128,768]{2,1,0:T(8,128)(2,1)S(1)} %fusion.41), channel_id=1, source_target_pairs={{0,8},{1,17},{2,10},{3,19},{4,12},{5,21},{6,14},{7,23},{8,0},{9,25... | collective-permute-start | bytes 589832 | tf_op jit(solution)/shard_map/ppermute | solution.py:93
  83.5 7.8 %collective-permute-start.13 = (bf16[2,128,768]{2,1,0:T(8,128)(2,1)S(1)}, bf16[2,128,768]{2,1,0:T(8,128)(2,1)S(1)}, u32[]{:S(2)}, u32[]{:S(2)}) collective-permute-start(bf16[2,128,768]{2,1,0:T(8,128)(2,1)S(1)} %pad_maximum_fusion.8), channel_id=1, source_target_pairs={{0,16},{1,9},{2,18},{3,11},{4,20},{5,13},{6,22},{7,15},{8,24},{9,1... | collective-permute-start | bytes 1179656 | tf_op jit(solution)/shard_map/ppermute | solution.py:93
  98.6 8.7 %collective-permute-start.20 = (bf16[2,128,768]{2,1,0:T(8,128)(2,1)}, bf16[2,128,768]{2,1,0:T(8,128)(2,1)}, u32[]{:S(2)}, u32[]{:S(2)}) collective-permute-start(bf16[2,128,768]{2,1,0:T(8,128)(2,1)} %bitcast.41), channel_id=1, source_target_pairs={{0,16},{1,9},{2,18},{3,11},{4,20},{5,13},{6,22},{7,15},{8,24},{9,1... | collective-permute-start | bytes 1179656 | tf_op jit(solution)/shard_map/ppermute | solution.py:93
  102.7 8.6 %collective-permute-start.18 = (bf16[2,128,768]{2,1,0:T(8,128)(2,1)}, bf16[2,128,768]{2,1,0:T(8,128)(2,1)}, u32[]{:S(2)}, u32[]{:S(2)}) collective-permute-start(bf16[2,128,768]{2,1,0:T(8,128)(2,1)} %bitcast.37), channel_id=1, source_target_pairs={{0,16},{1,9},{2,18},{3,11},{4,20},{5,13},{6,22},{7,15},{8,24},{9,1... | collective-permute-start | bytes 1179656 | tf_op jit(solution)/shard_map/ppermute | solution.py:93
  109.5 5.7 %collective-permute-start.21 = (bf16[1,128,768]{2,1,0:T(8,128)(2,1)S(1)}, bf16[1,128,768]{2,1,0:T(8,128)(2,1)S(1)}, u32[]{:S(2)}, u32[]{:S(2)}) collective-permute-start(bf16[1,128,768]{2,1,0:T(8,128)(2,1)S(1)} %slice.386), channel_id=1, source_target_pairs={{0,8},{1,17},{2,10},{3,19},{4,12},{5,21},{6,14},{7,23},{8,0},{9,25... | collective-permute-start | bytes 589832 | tf_op jit(solution)/shard_map/ppermute | solution.py:93
  112.5 5.7 %collective-permute-start.19 = (bf16[1,128,768]{2,1,0:T(8,128)(2,1)S(1)}, bf16[1,128,768]{2,1,0:T(8,128)(2,1)S(1)}, u32[]{:S(2)}, u32[]{:S(2)}) collective-permute-start(bf16[1,128,768]{2,1,0:T(8,128)(2,1)S(1)} %slice.387), channel_id=1, source_target_pairs={{0,8},{1,17},{2,10},{3,19},{4,12},{5,21},{6,14},{7,23},{8,0},{9,25... | collective-permute-start | bytes 589832 | tf_op jit(solution)/shard_map/ppermute | solution.py:93
  120.7 5.0 %collective-permute-start.22 = (bf16[2,1,128,192]{3,2,0,1:T(8,128)(2,1)S(1)}, bf16[2,1,128,192]{3,2,0,1:T(8,128)(2,1)S(1)}, u32[]{:S(2)}, u32[]{:S(2)}) collective-permute-start(bf16[2,1,128,192]{3,2,0,1:T(8,128)(2,1)S(1)} %get-tuple-element.110), channel_id=1, source_target_pairs={{0,8},{1,17},{2,10},{3,19},{4,12},{5,21},{6,14},{7,23},{8,0},{9,25... | collective-permute-start | bytes 294920 | tf_op jit(solution)/shard_map/ppermute | solution.py:93
  123.2 31.0 %collective-permute-start.44 = (bf16[4,96,1536]{2,1,0:T(8,128)(2,1)}, bf16[4,96,1536]{2,1,0:T(8,128)(2,1)}, u32[]{:S(2)}, u32[]{:S(2)}) collective-permute-start(bf16[4,96,1536]{2,1,0:T(8,128)(2,1)} %fusion.13), channel_id=1, source_target_pairs={{0,1},{1,0},{2,3},{3,2},{4,5},{5,4},{6,7},{7,6},{8,9},{9,8},{10,11... | collective-permute-start | bytes 3538952 | tf_op jit(solution)/shard_map/ppermute | solution.py:82
  125.8 5.0 %collective-permute-start.23 = (bf16[1,2,128,192]{3,2,1,0:T(8,128)(2,1)S(1)}, bf16[1,2,128,192]{3,2,1,0:T(8,128)(2,1)S(1)}, u32[]{:S(2)}, u32[]{:S(2)}) collective-permute-start(bf16[1,2,128,192]{3,2,1,0:T(8,128)(2,1)S(1)} %get-tuple-element.108), channel_id=1, source_target_pairs={{0,16},{1,9},{2,18},{3,11},{4,20},{5,13},{6,22},{7,15},{8,24},{9,1... | collective-permute-start | bytes 294920 | tf_op jit(solution)/shard_map/ppermute | solution.py:93
  139.9 8.1 %collective-permute-start.24 = (bf16[2,128,768]{2,1,0:T(8,128)(2,1)}, bf16[2,128,768]{2,1,0:T(8,128)(2,1)}, u32[]{:S(2)}, u32[]{:S(2)}) collective-permute-start(bf16[2,128,768]{2,1,0:T(8,128)(2,1)} %get-tuple-element.42), channel_id=1, source_target_pairs={{0,16},{1,9},{2,18},{3,11},{4,20},{5,13},{6,22},{7,15},{8,24},{9,1... | collective-permute-start | bytes 1179656 | tf_op jit(solution)/shard_map/ppermute | solution.py:93
  142.7 7.3 %collective-permute-start.38 = (bf16[4,96,768]{2,1,0:T(8,128)(2,1)}, bf16[4,96,768]{2,1,0:T(8,128)(2,1)}, u32[]{:S(2)}, u32[]{:S(2)}) collective-permute-start(bf16[4,96,768]{2,1,0:T(8,128)(2,1)} %fusion.22), channel_id=1, source_target_pairs={{0,1},{1,0},{2,3},{3,2},{4,5},{5,4},{6,7},{7,6},{8,9},{9,8},{10,11... | collective-permute-start | bytes 1769480 | tf_op jit(solution)/shard_map/ppermute | solution.py:82
  144.1 17.3 %collective-permute-start.32 = (bf16[4,96,576]{2,1,0:T(8,128)(2,1)}, bf16[4,96,576]{2,1,0:T(8,128)(2,1)}, u32[]{:S(2)}, u32[]{:S(2)}) collective-permute-start(bf16[4,96,576]{2,1,0:T(8,128)(2,1)} %get-tuple-element.48), channel_id=1, source_target_pairs={{0,1},{1,0},{2,3},{3,2},{4,5},{5,4},{6,7},{7,6},{8,9},{9,8},{10,11... | collective-permute-start | bytes 1327112 | tf_op jit(solution)/shard_map/ppermute | solution.py:82
  149.3 8.7 %collective-permute-start.25 = (bf16[1,128,768]{2,1,0:T(8,128)(2,1)S(1)}, bf16[1,128,768]{2,1,0:T(8,128)(2,1)S(1)}, u32[]{:S(2)}, u32[]{:S(2)}) collective-permute-start(bf16[1,128,768]{2,1,0:T(8,128)(2,1)S(1)} %slice.385), channel_id=1, source_target_pairs={{0,8},{1,17},{2,10},{3,19},{4,12},{5,21},{6,14},{7,23},{8,0},{9,25... | collective-permute-start | bytes 589832 | tf_op jit(solution)/shard_map/ppermute | solution.py:93
  152.1 20.3 %collective-permute-start.41 = (bf16[96,768]{1,0:T(8,128)(2,1)}, bf16[96,768]{1,0:T(8,128)(2,1)}, u32[]{:S(2)}, u32[]{:S(2)}) collective-permute-start(bf16[96,768]{1,0:T(8,128)(2,1)} %get-tuple-element.97), channel_id=1, source_target_pairs={{0,6},{1,7},{2,4},{3,5},{4,2},{5,3},{6,0},{7,1},{8,14},{9,15},{10,... | collective-permute-start | bytes 442376 | tf_op jit(solution)/shard_map/ppermute | solution.py:82
  154.2 19.5 %collective-permute-start.40 = (bf16[96,768]{1,0:T(8,128)(2,1)}, bf16[96,768]{1,0:T(8,128)(2,1)}, u32[]{:S(2)}, u32[]{:S(2)}) collective-permute-start(bf16[96,768]{1,0:T(8,128)(2,1)} %get-tuple-element.98), channel_id=1, source_target_pairs={{0,4},{1,5},{2,6},{3,7},{4,0},{5,1},{6,2},{7,3},{8,12},{9,13},{10,... | collective-permute-start | bytes 442376 | tf_op jit(solution)/shard_map/ppermute | solution.py:82
  162.9 5.5 %collective-permute-start.29 = (bf16[12,96]{1,0:T(8,128)(2,1)S(1)}, bf16[12,96]{1,0:T(8,128)(2,1)S(1)}, u32[]{:S(2)}, u32[]{:S(2)}) collective-permute-start(bf16[12,96]{1,0:T(8,128)(2,1)S(1)} %get-tuple-element.118), channel_id=1, source_target_pairs={{0,6},{1,7},{2,4},{3,5},{4,2},{5,3},{6,0},{7,1},{8,14},{9,15},{10,... | collective-permute-start | bytes 6920 | tf_op jit(solution)/shard_map/ppermute | solution.py:82
  164.7 4.5 %collective-permute-start.28 = (bf16[12,96]{1,0:T(8,128)(2,1)S(1)}, bf16[12,96]{1,0:T(8,128)(2,1)S(1)}, u32[]{:S(2)}, u32[]{:S(2)}) collective-permute-start(bf16[12,96]{1,0:T(8,128)(2,1)S(1)} %get-tuple-element.119), channel_id=1, source_target_pairs={{0,4},{1,5},{2,6},{3,7},{4,0},{5,1},{6,2},{7,3},{8,12},{9,13},{10,... | collective-permute-start | bytes 6920 | tf_op jit(solution)/shard_map/ppermute | solution.py:82
  166.7 4.6 %collective-permute-start.27 = (bf16[12,96]{1,0:T(8,128)(2,1)S(1)}, bf16[12,96]{1,0:T(8,128)(2,1)S(1)}, u32[]{:S(2)}, u32[]{:S(2)}) collective-permute-start(bf16[12,96]{1,0:T(8,128)(2,1)S(1)} %get-tuple-element.117), channel_id=1, source_target_pairs={{0,2},{1,3},{2,0},{3,1},{4,6},{5,7},{6,4},{7,5},{8,10},{9,11},{10,... | collective-permute-start | bytes 6920 | tf_op jit(solution)/shard_map/ppermute | solution.py:82
  168.4 7.4 %collective-permute-start.39 = (bf16[96,768]{1,0:T(8,128)(2,1)S(1)}, bf16[96,768]{1,0:T(8,128)(2,1)S(1)}, u32[]{:S(2)}, u32[]{:S(2)}) collective-permute-start(bf16[96,768]{1,0:T(8,128)(2,1)S(1)} %copy-done.42), channel_id=1, source_target_pairs={{0,2},{1,3},{2,0},{3,1},{4,6},{5,7},{6,4},{7,5},{8,10},{9,11},{10,... | collective-permute-start | bytes 442376 | tf_op jit(solution)/shard_map/ppermute | solution.py:82
  169.2 44.5 %collective-permute-start.47 = (bf16[96,1536]{1,0:T(8,128)(2,1)S(1)}, bf16[96,1536]{1,0:T(8,128)(2,1)S(1)}, u32[]{:S(2)}, u32[]{:S(2)}) collective-permute-start(bf16[96,1536]{1,0:T(8,128)(2,1)S(1)} %copy-done.36), channel_id=1, source_target_pairs={{0,6},{1,7},{2,4},{3,5},{4,2},{5,3},{6,0},{7,1},{8,14},{9,15},{10,... | collective-permute-start | bytes 884744 | tf_op jit(solution)/shard_map/ppermute | solution.py:82
  171.3 42.4 %collective-permute-start.46 = (bf16[96,1536]{1,0:T(8,128)(2,1)S(1)}, bf16[96,1536]{1,0:T(8,128)(2,1)S(1)}, u32[]{:S(2)}, u32[]{:S(2)}) collective-permute-start(bf16[96,1536]{1,0:T(8,128)(2,1)S(1)} %get-tuple-element.92), channel_id=1, source_target_pairs={{0,4},{1,5},{2,6},{3,7},{4,0},{5,1},{6,2},{7,3},{8,12},{9,13},{10,... | collective-permute-start | bytes 884744 | tf_op jit(solution)/shard_map/ppermute | solution.py:82
  172.5 41.3 %collective-permute-start.45 = (bf16[96,1536]{1,0:T(8,128)(2,1)S(1)}, bf16[96,1536]{1,0:T(8,128)(2,1)S(1)}, u32[]{:S(2)}, u32[]{:S(2)}) collective-permute-start(bf16[96,1536]{1,0:T(8,128)(2,1)S(1)} %get-tuple-element.90), channel_id=1, source_target_pairs={{0,2},{1,3},{2,0},{3,1},{4,6},{5,7},{6,4},{7,5},{8,10},{9,11},{10,... | collective-permute-start | bytes 884744 | tf_op jit(solution)/shard_map/ppermute | solution.py:82
  173.7 22.4 %collective-permute-start.35 = (bf16[96,576]{1,0:T(8,128)(2,1)S(1)}, bf16[96,576]{1,0:T(8,128)(2,1)S(1)}, u32[]{:S(2)}, u32[]{:S(2)}) collective-permute-start(bf16[96,576]{1,0:T(8,128)(2,1)S(1)} %get-tuple-element.100), channel_id=1, source_target_pairs={{0,6},{1,7},{2,4},{3,5},{4,2},{5,3},{6,0},{7,1},{8,14},{9,15},{10,... | collective-permute-start | bytes 331784 | tf_op jit(solution)/shard_map/ppermute | solution.py:82
  175.8 27.6 %collective-permute-start.30 = (bf16[1,12,96]{2,1,0:T(8,128)(2,1)S(1)}, bf16[1,12,96]{2,1,0:T(8,128)(2,1)S(1)}, u32[]{:S(2)}, u32[]{:S(2)}) collective-permute-start(bf16[1,12,96]{2,1,0:T(8,128)(2,1)S(1)} %fusion.50), channel_id=1, source_target_pairs={{0,8},{1,17},{2,10},{3,19},{4,12},{5,21},{6,14},{7,23},{8,0},{9,25... | collective-permute-start | bytes 6920 | tf_op jit(solution)/shard_map/ppermute | solution.py:93
  196.1 11.1 %collective-permute-start.34 = (bf16[96,576]{1,0:T(8,128)(2,1)S(1)}, bf16[96,576]{1,0:T(8,128)(2,1)S(1)}, u32[]{:S(2)}, u32[]{:S(2)}) collective-permute-start(bf16[96,576]{1,0:T(8,128)(2,1)S(1)} %get-tuple-element.101), channel_id=1, source_target_pairs={{0,4},{1,5},{2,6},{3,7},{4,0},{5,1},{6,2},{7,3},{8,12},{9,13},{10,... | collective-permute-start | bytes 331784 | tf_op jit(solution)/shard_map/ppermute | solution.py:82
  203.4 5.3 %collective-permute-start.33 = (bf16[96,576]{1,0:T(8,128)(2,1)S(1)}, bf16[96,576]{1,0:T(8,128)(2,1)S(1)}, u32[]{:S(2)}, u32[]{:S(2)}) collective-permute-start(bf16[96,576]{1,0:T(8,128)(2,1)S(1)} %get-tuple-element.99), channel_id=1, source_target_pairs={{0,2},{1,3},{2,0},{3,1},{4,6},{5,7},{6,4},{7,5},{8,10},{9,11},{10,... | collective-permute-start | bytes 331784 | tf_op jit(solution)/shard_map/ppermute | solution.py:82
  207.1 12.5 %collective-permute-start.42 = (bf16[1,96,768]{2,1,0:T(8,128)(2,1)S(1)}, bf16[1,96,768]{2,1,0:T(8,128)(2,1)S(1)}, u32[]{:S(2)}, u32[]{:S(2)}) collective-permute-start(bf16[1,96,768]{2,1,0:T(8,128)(2,1)S(1)} %fusion.42), channel_id=1, source_target_pairs={{0,8},{1,17},{2,10},{3,19},{4,12},{5,21},{6,14},{7,23},{8,0},{9,25... | collective-permute-start | bytes 442376 | tf_op jit(solution)/shard_map/ppermute | solution.py:93
  212.4 6.2 %collective-permute-start.36 = (bf16[1,96,576]{2,1,0:T(8,128)(2,1)S(1)}, bf16[1,96,576]{2,1,0:T(8,128)(2,1)S(1)}, u32[]{:S(2)}, u32[]{:S(2)}) collective-permute-start(bf16[1,96,576]{2,1,0:T(8,128)(2,1)S(1)} %bitcast.273), channel_id=1, source_target_pairs={{0,8},{1,17},{2,10},{3,19},{4,12},{5,21},{6,14},{7,23},{8,0},{9,25... | collective-permute-start | bytes 331784 | tf_op jit(solution)/shard_map/ppermute | solution.py:93
  215.0 9.9 %collective-permute-start.48 = (bf16[1,96,1536]{2,1,0:T(8,128)(2,1)S(1)}, bf16[1,96,1536]{2,1,0:T(8,128)(2,1)S(1)}, u32[]{:S(2)}, u32[]{:S(2)}) collective-permute-start(bf16[1,96,1536]{2,1,0:T(8,128)(2,1)S(1)} %bitcast.256), channel_id=1, source_target_pairs={{0,8},{1,17},{2,10},{3,19},{4,12},{5,21},{6,14},{7,23},{8,0},{9,25... | collective-permute-start | bytes 884744 | tf_op jit(solution)/shard_map/ppermute | solution.py:93
  218.6 8.1 %collective-permute-start.37 = (bf16[2,96,576]{2,1,0:T(8,128)(2,1)S(1)}, bf16[2,96,576]{2,1,0:T(8,128)(2,1)S(1)}, u32[]{:S(2)}, u32[]{:S(2)}) collective-permute-start(bf16[2,96,576]{2,1,0:T(8,128)(2,1)S(1)} %pad_maximum_fusion.13), channel_id=1, source_target_pairs={{0,16},{1,9},{2,18},{3,11},{4,20},{5,13},{6,22},{7,15},{8,24},{9,1... | collective-permute-start | bytes 663560 | tf_op jit(solution)/shard_map/ppermute | solution.py:93
  220.4 10.0 %collective-permute-start.43 = (bf16[2,96,768]{2,1,0:T(8,128)(2,1)}, bf16[2,96,768]{2,1,0:T(8,128)(2,1)}, u32[]{:S(2)}, u32[]{:S(2)}) collective-permute-start(bf16[2,96,768]{2,1,0:T(8,128)(2,1)} %pad_maximum_fusion.9), channel_id=1, source_target_pairs={{0,16},{1,9},{2,18},{3,11},{4,20},{5,13},{6,22},{7,15},{8,24},{9,1... | collective-permute-start | bytes 884744 | tf_op jit(solution)/shard_map/ppermute | solution.py:93
  225.8 10.1 %collective-permute-start.49 = (bf16[2,96,1536]{2,1,0:T(8,128)(2,1)}, bf16[2,96,1536]{2,1,0:T(8,128)(2,1)S(1)}, u32[]{:S(2)}, u32[]{:S(2)}) collective-permute-start(bf16[2,96,1536]{2,1,0:T(8,128)(2,1)} %pad_maximum_fusion.6), channel_id=1, source_target_pairs={{0,16},{1,9},{2,18},{3,11},{4,20},{5,13},{6,22},{7,15},{8,24},{9,1... | collective-permute-start | bytes 1769480 | tf_op jit(solution)/shard_map/ppermute | solution.py:93
  (55 other events, 337.7 us)

commit v2 on v1

--- a/solution.py
+++ b/solution.py
@@ -5,8 +5,10 @@
 from jax.experimental.pallas import tpu as pltpu
 from jax.sharding import PartitionSpec as P
 
+
 HEADS = 12
 HEAD = 64
+
 
 EPS = 1e-05
 GELU_C = 0.7978845608028654
@@ -97,11 +99,16 @@
     return range(group_size().bit_length() - 1)
 
 
+def gather_halves(block):
+    held, moved = None, block[None]
+    for level in sides():
+        held = moved if held is None else jnp.concatenate([held, moved], axis=0)
+        moved = to_side(held, level)
+    return held, moved
+
+
 def gather_side(block):
-    held = block[None]
-    for level in sides():
-        held = jnp.concatenate([held, to_side(held, level)], axis=0)
-    return held
+    return jnp.concatenate(gather_halves(block), axis=0)
 
 
 def reduce_side(low, high):
@@ -110,26 +117,23 @@
         if high is None:
             half = total.shape[0] // 2
             total, high = total[:half], total[half:].astype(BF)
-        total = total + to_side(high, level).astype(F32)
+        moved = to_side(high, level)
+        total = total + moved.astype(F32)
         high = None
     return total[0]
 
 
-def in_order(blocks, me):
-    bits = group_size().bit_length() - 1
-    core = lax.axis_index("shard") & 1
-    if bits == 2:
+def in_order(blocks, me, core):
+    if len(blocks) == 4:
         first, second = blocks[1], blocks[2]
         blocks = [blocks[0], jnp.where(core == 0, first, second),
                   jnp.where(core == 0, second, first), blocks[3]]
     return swap_by_index(blocks, me)
 
 
-def from_order(blocks, me):
-    bits = group_size().bit_length() - 1
-    core = lax.axis_index("shard") & 1
+def from_order(blocks, me, core):
     blocks = swap_by_index(blocks, me)
-    if bits == 2:
+    if len(blocks) == 4:
         first, second = blocks[1], blocks[2]
         blocks = [blocks[0], jnp.where(core == 0, first, second),
                   jnp.where(core == 0, second, first), blocks[3]]
@@ -209,7 +213,6 @@
 
 
 def pack_mlp_kernel(at_ref, up_ref, down_ref, out_ref):
-    rows = up_ref.shape[0]
     hid = down_ref.shape[0]
     ranks = up_ref.shape[1] // (out_ref.shape[1] - down_ref.shape[1])
     part = hid // ranks
@@ -232,21 +235,30 @@
     out_ref[2 * tokens:2 * tokens + 16] = jnp.broadcast_to(line, (16, width)).astype(BF)
 
 
-def attend_kernel(_, all_ref, w_ref, gain_ref, shift_ref, bias_ref,
-                  normed_ref, dm_ref, packed_ref, p_ref, out_ref):
+def attend_kernel(at_ref, low_ref, high_ref, w_ref, vec_ref,
+                  normed_ref, dm_ref, packed_ref, p_ref, out_ref, lines_ref, hid_ref):
     ranks, tokens, part = out_ref.shape
     heads = part // HEAD
-    gain, shift = gain_ref[...], shift_ref[...]
+    shards, count, rows = vec_ref.shape
+    me = at_ref[0]
+    lines = jnp.concatenate([vec_ref[s] for s in range(shards)], axis=1)
+    lines_ref[...] = lines[0:8]
+    hid_ref[...] = choose(me, [lines[8 + i:9 + i] for i in range(count - 8)])
+    gain, shift = lines[0:1], lines[1:2]
+    bias = [choose(me, [lines[j:j + 1, i * part:(i + 1) * part] for i in range(ranks)])
+            for j in (2, 3)]
+    bias = jnp.concatenate([bias[0], jnp.zeros((1, part), F32), bias[1]], axis=1)
+    sources = [ref.at[i] for ref in (low_ref, high_ref) for i in range(ranks // 2)]
     for g in range(ranks):
         span = slice(g * tokens, (g + 1) * tokens)
-        normed_ref[span] = (all_ref[g, 0:tokens].astype(F32) * gain + shift).astype(BF)
-        dm_ref[span] = all_ref[g, tokens:2 * tokens]
-    packed_ref[...] = (mm(normed_ref[...], w_ref[...]) + bias_ref[...]).astype(BF)
+        normed_ref[span] = (sources[g][0:tokens].astype(F32) * gain + shift).astype(BF)
+        dm_ref[span] = sources[g][tokens:2 * tokens]
+    packed_ref[...] = (mm(normed_ref[...], w_ref[...]) + bias).astype(BF)
     rows = lax.broadcasted_iota(jnp.int32, (tokens, tokens), 0)
     columns = lax.broadcasted_iota(jnp.int32, (tokens, tokens), 1)
     for g in range(ranks):
         span = slice(g * tokens, (g + 1) * tokens)
-        line = all_ref[g, 2 * tokens:2 * tokens + 16, 0:tokens].astype(F32)[0:1]
+        line = sources[g][2 * tokens:2 * tokens + 16, 0:tokens].astype(F32)[0:1]
         across = jnp.broadcast_to(line, (tokens, tokens))
         allowed = (rows >= columns) & (across == across.T)
         for h in range(heads):
@@ -299,6 +311,29 @@
         other_ref[i] = jnp.where(even, second, first).astype(BF)
 
 
+def unpack_qkv_kernel(at_ref, low_ref, high_ref, out_ref):
+    half, _, columns = low_ref.shape
+    part = columns // 3
+    blocks = [ref[i] for ref in (low_ref, high_ref) for i in range(half)]
+    blocks = in_order(blocks, at_ref[1], at_ref[0])
+    out_ref[...] = jnp.concatenate(
+        [one[:, j * part:(j + 1) * part].astype(F32) for j in range(3) for one in blocks], axis=1)
+
+
+def unpack_mlp_kernel(at_ref, low_ref, high_ref, up_ref, down_ref):
+    half, _, columns = low_ref.shape
+    width = down_ref.shape[1]
+    ranks = 2 * half
+    per = down_ref.shape[0] // ranks
+    blocks = [ref[i] for ref in (low_ref, high_ref) for i in range(half)]
+    blocks = in_order(blocks, at_ref[1], at_ref[0])
+    for r, one in enumerate(blocks):
+        down_ref[r * per:(r + 1) * per] = one[:, columns - width:].astype(F32)
+    for s in range((columns - width) // per):
+        up_ref[:, s * ranks * per:(s + 1) * ranks * per] = jnp.concatenate(
+            [one[:, s * per:(s + 1) * per].astype(F32) for one in blocks], axis=1)
+
+
 def finish_kernel(at_ref, hidden_ref, grad_ref, middle_ref, gain_ref, bias_ref, hid_ref, rest_ref,
                   input_ref, mine_ref, other_ref):
     unit, scale = norm_parts(hidden_ref[...])
@@ -343,12 +378,14 @@
 def reduce_shard(mine, other):
     links = mine.shape[0]
     place = lax.axis_index("shard") >> 1
-    mine = mine + to_shard(other, 1).astype(F32)
+    moved = to_shard(other, 1)
+    mine = mine + moved.astype(F32)
     total = lax.dynamic_index_in_dim(mine, place, 0, keepdims=False)
     mine = mine.astype(BF)
     for step in range(1, links):
         block = lax.dynamic_index_in_dim(mine, place ^ step, 0, keepdims=False)
-        total = total + to_shard(block, 2 * step).astype(F32)
+        moved = to_shard(block, 2 * step)
+        total = total + moved.astype(F32)
     step = group_size()
     while step < lax.axis_size("rep"):
         total = total + to_rep(total.astype(BF), step).astype(F32)
@@ -378,9 +415,10 @@
     count = 8 + hid_rows // rows
     sent, = call(start_kernel, mine, (hidden, cotangent, doc_ids),
                  [((2 * tokens + 16, width), BF)])
-    w_qkv, = call(pack_kernel, mine, [qkv_weight[0]] + vectors, [((rows + count, 3 * part), BF)])
+    lines = -(-(rows + count) // 16) * 16
+    w_qkv, = call(pack_kernel, mine, [qkv_weight[0]] + vectors, [((lines, 3 * part), BF)])
     qkv_links = gather_links(w_qkv)
-    every = gather_side(sent)
+    every_low, every_high = gather_halves(sent)
     w_qkv, vec = gather_pair(qkv_links, ((rows, 3 * part), BF), ((count, rows), F32))
     w_qkv = w_qkv.reshape(width, 3 * part)
     w_out = after(out_weight[0].astype(BF), *qkv_links)
@@ -389,33 +427,25 @@
     w_out = w_out.reshape(width, width)
     w_mlp, = call(pack_mlp_kernel, mine, (up_weight[0], down_weight[0]),
                   [((rows, shards * hid_part + width), BF)])
-    mlp_links = gather_links(after(w_mlp, *out_links))
+    whole = ranks * tokens
+    normed_all, grad_down_all, packed, weights, mixed, lines, u_bias = call(
+        attend_kernel, mine, (every_low, every_high, w_qkv, vec),
+        [((whole, width), BF), ((whole, width), BF), ((whole, 3 * part), BF),
+         ((ranks * heads, tokens, tokens), F32), ((ranks, tokens, part), BF),
+         ((8, width), F32), ((1, shards * hid_part), F32)])
+    p_gain, _, _, _, o_bias, s_gain, s_shift, d_bias = [lines[i:i + 1] for i in range(8)]
+    mlp_links = gather_links(after(w_mlp, w_qkv))
+    mixed = exchange_side([mixed[i] for i in range(ranks)])
+    mixed = jnp.concatenate(in_order([mixed[i] for i in range(ranks)], me, core), axis=1)
+    middle = hidden + mm(mixed, w_out) + o_bias
+    unit2, scale2 = norm_parts(middle)
+    normed_two = (unit2 * s_gain + s_shift).astype(BF)
+    two_low, two_high = gather_halves(normed_two)
+    normed_two_all = jnp.concatenate([two_low, two_high], axis=0).reshape(whole, width)
+    mlp_links = lax.optimization_barrier((*mlp_links, two_low))[:-1]
     w_mlp, = gather_pair(mlp_links, ((rows, shards * hid_part + width), BF))
     w_mlp = w_mlp.reshape(width, -1)
     w_up, w_down = w_mlp[:, :shards * hid_part], w_mlp[:, shards * hid_part:]
-
-    lines = vec.transpose(1, 0, 2)
-    p_gain, p_shift, q_bias, v_bias, o_bias, s_gain, s_shift, d_bias = [
-        lines[i].reshape(1, width) for i in range(8)
-    ]
-    hid_bias = lines[8:].transpose(1, 0, 2).reshape(shards, ranks, hid_part)
-    u_bias = lax.dynamic_index_in_dim(hid_bias, me, 1, keepdims=False).reshape(1, -1)
-
-    def quarter(vector):
-        return lax.dynamic_slice_in_dim(vector, me * part, part, 1)
-
-    bias_row = jnp.concatenate([quarter(q_bias), jnp.zeros((1, part), F32), quarter(v_bias)], axis=1)
-    whole = ranks * tokens
-    normed_all, grad_down_all, packed, weights, mixed = call(
-        attend_kernel, mine, (every, w_qkv, p_gain, p_shift, bias_row),
-        [((whole, width), BF), ((whole, width), BF), ((whole, 3 * part), BF),
-         ((ranks * heads, tokens, tokens), F32), ((ranks, tokens, part), BF)])
-    mixed = exchange_side([mixed[i] for i in range(ranks)])
-    mixed = jnp.concatenate(in_order([mixed[i] for i in range(ranks)], me), axis=1)
-    middle = hidden + mm(mixed, w_out) + o_bias
-    unit2, scale2 = norm_parts(middle)
-    normed_two = (unit2 * s_gain + s_shift).astype(BF)
-    normed_two_all = gather_side(normed_two).reshape(whole, width)
     pre_act = mm(normed_two_all, w_up) + u_bias
     activ, slope = gelu_and_slope(pre_act)
     activ = activ.astype(BF)
@@ -430,7 +460,7 @@
     grad_attn = grad_middle.astype(BF)
     grad_mixed = mm_nt(grad_attn, w_out).astype(BF)
     blocks = [grad_mixed[:, i * part:(i + 1) * part] for i in range(ranks)]
-    grad_mixed = exchange_side(from_order(blocks, me))
+    grad_mixed = exchange_side(from_order(blocks, me, core))
     links = shards // 2
     low, high, qkv_mine, qkv_other, bias_sums, _ = call(
         attend_back_kernel, at, (packed, weights, grad_mixed, normed_all, w_qkv),
@@ -440,27 +470,26 @@
     grad_one = reduce_side(low, high)
 
     sum_out = mm(activ, w_down).reshape(ranks, tokens, width)
-    hidden_out = reduce_side(sum_out[:half], sum_out[half:].astype(BF)) + (middle + d_bias)
+    hidden_out = reduce_side(
+        sum_out[:half], after(sum_out[half:].astype(BF), grad_mixed)) + (middle + d_bias)
 
     def by_shard(grad):
         return grad.reshape(shards, rows, -1)
 
-    def every_rep(block):
-        held = gather_side(block)
-        return jnp.stack(in_order([held[i] for i in range(ranks)], me))
-
     g_mlp = reduce_shard(*split_shard(jnp.concatenate(
         [by_shard(mm_tn(normed_two_all, grad_pre)), by_shard(mm_tn(activ, grad_down_all))], axis=2)))
-    g_mlp = every_rep(g_mlp)
-    g_up = g_mlp[:, :, :shards * hid_part].astype(F32).reshape(ranks, rows, shards, hid_part)
-    g_up = g_up.transpose(1, 2, 0, 3).reshape(1, rows, -1)
-    g_down = g_mlp[:, :, shards * hid_part:].astype(F32).reshape(1, hid_rows, width)
+    g_mlp = gather_halves(g_mlp)
+    g_up, g_down = call(
+        unpack_mlp_kernel, at, g_mlp,
+        [((rows, ranks * shards * hid_part), F32), ((hid_rows, width), F32)])
+    g_up, g_down = g_up[None], g_down[None]
 
     g_out = reduce_shard(*split_shard(by_shard(mm_tn(mixed, grad_attn))))
     g_out = jnp.sum(gather_side(g_out).astype(F32), axis=0)[None]
 
-    g_qkv = every_rep(reduce_shard(qkv_mine, qkv_other)).astype(F32)
-    g_qkv = g_qkv.reshape(ranks, rows, 3, part).transpose(1, 2, 0, 3).reshape(1, rows, -1)
+    g_qkv = gather_halves(reduce_shard(qkv_mine, qkv_other))
+    g_qkv, = call(unpack_qkv_kernel, at, g_qkv, [((rows, 3 * width), F32)])
+    g_qkv = g_qkv[None]
 
     rest = jnp.concatenate([
         jnp.sum(grad_attn.astype(F32), axis=0, keepdims=True), g_s_gain, g_s_shift,
@@ -485,6 +514,7 @@
         vector, vector, matrix, vector, matrix, vector,
     )
     out_specs = (tokens, tokens) + in_specs[3:]
+
     return jax.shard_map(
         split_plan, mesh=mesh, in_specs=in_specs, out_specs=out_specs, check_vma=False
     )

time: 244 us -> 236 us (0.967)
  local copies, waits for them, and re-layouts: 29.4 us -> 8.96 us
  starting transfers between devices: 57.8 us -> 69.5 us
  waiting for transfers between devices: 75.7 us -> 85.2 us
  other arithmetic: 30.7 us -> 21.7 us
  Pallas kernels: 33.8 us -> 39.7 us
  matrix products: 13.6 us -> 8.99 us
    ppermute x28, waiting for transfers between devices: 41.4 us -> 48.8 us  [to_shard(): lax.ppermute(block, 'shard', [(one, one ^ step) for one in range(count)])]
    reshape x5 -> x0, local copies, waits for them, and re-layouts: 7.09 us -> none  [the longest x3 4.36 us: split_plan(): g_up = g_up.transpose(1, 2, 0, 3).reshape(1, rows, -1)]
    ppermute x28, starting transfers between devices: 34.8 us -> 41.4 us  [to_shard(): lax.ppermute(block, 'shard', [(one, one ^ step) for one in range(count)])]
    pallas_call x6 -> x8, Pallas kernels: 26 us -> 31.8 us  [call(): pl.pallas_call(kernel, out_shape=[jax.ShapeDtypeStruct(shape, dtype) for...]
    ppermute x22, starting transfers between devices: 23 us -> 28.2 us  [to_side(): return lax.ppermute(block, ('rep', 'shard'), pairs)]
    dot_general x3, matrix products: 6.47 us -> 2.45 us  [mm_tn(): lax.dot_general(left, right, (((0,), (0,)), ((), ())), preferred_element_...]
    another operation x6 -> x0, local copies, waits for them, and re-layouts: 2.52 us -> none  [the longest x4 1.48 us: split_plan(): lines[i].reshape(1, width)]
  transfers between devices with their start and end apart: 50 -> 50, of which waited for: 21 -> 21; matrix products, arithmetic and copies ran while one was open for 22% -> 12% of each run, Pallas kernels for 13% -> 13%
where the time goes in v2:
time: 236 us
  waiting for transfers between devices  85.2 us (36%)
  starting transfers between devices  69.5 us (29%)
  Pallas kernels  39.7 us (17%)
  other arithmetic  21.7 us (9%)
  matrix products  8.99 us (4%)
  local copies, waits for them, and re-layouts  8.96 us (4%)
    ppermute x28, waiting for transfers between devices, to_shard(): lax.ppermute(block, 'shard', [(one, one ^ step) for one in range(count)])  48.8 us
    ppermute x28, starting transfers between devices, to_shard(): lax.ppermute(block, 'shard', [(one, one ^ step) for one in range(count)])  41.4 us
    ppermute x22, waiting for transfers between devices, to_side(): return lax.ppermute(block, ('rep', 'shard'), pairs)  36.4 us
    pallas_call x8, Pallas kernels, call(): pl.pallas_call(kernel, out_shape=[jax.ShapeDtypeStruct(shape, dtype) for...  31.8 us
    ppermute x22, starting transfers between devices, to_side(): return lax.ppermute(block, ('rep', 'shard'), pairs)  28.2 us
    pallas_call x3, Pallas kernels, gather_pair(): pl.pallas_call(place_kernel, out_shape=[jax.ShapeDtypeStruct((count,) + s...  7.91 us
    convert_element_type x4, other arithmetic, reduce_shard(): mine = mine.astype(BF)  6.89 us
  transfers between devices with their start and end apart: 50, of which 21 were waited for; matrix products, arithmetic and copies ran while one was open for 12% of the time, Pallas kernels for 13%

profile of v2, /device:TPU:0, one launch (start us, length us, event | category | flops | bytes accessed | tf_op | source)
XLA Modules:
  0.0 235.6 jit_solution(5465154616148416454)
XLA Ops:
  0.7 2.1 shard_map.271
  2.7 3.0 %collective-permute-start = (bf16[1,272,768]{2,1,0:T(8,128)(2,1)}, bf16[1,272,768]{2,1,0:T(8,128)(2,1)S(1)}, u32[]{:S(2)}, u32[]{:S(2)}) collective-permute-start(bf16[1,272,768]{2,1,0:T(8,128)(2,1)} %bitcast.213), channel_id=1, source_target_pairs={{0,8},{1,17},{2,10},{3,19},{4,12},{5,21},{6,14},{7,23},{8,0},{9,25... | collective-permute-start | bytes 1253384 | tf_op jit(solution)/shard_map/ppermute | solution.py:95
  5.7 2.3 shard_map.272
  8.0 3.6 %collective-permute-start.4 = (bf16[112,576]{1,0:T(8,128)(2,1)}, bf16[112,576]{1,0:T(8,128)(2,1)S(1)}, u32[]{:S(2)}, u32[]{:S(2)}) collective-permute-start(bf16[112,576]{1,0:T(8,128)(2,1)} %shard_map.272), channel_id=1, source_target_pairs={{0,6},{1,7},{2,4},{3,5},{4,2},{5,3},{6,0},{7,1},{8,14},{9,15},{10,... | collective-permute-start | bytes 387080 | tf_op jit(solution)/shard_map/ppermute | solution.py:84
  16.7 7.0 %collective-permute-done.3 = bf16[112,576]{1,0:T(8,128)(2,1)S(1)} collective-permute-done((bf16[112,576]{1,0:T(8,128)(2,1)}, bf16[112,576]{1,0:T(8,128)(2,1)S(1)}, u32[]{:S(2)}, u32[]{:S(2)}) %collective-permute-start.3) | collective-permute-done | bytes 129056 | tf_op jit(solution)/shard_map/ppermute | solution.py:84
  23.7 2.7 %collective-permute-start.10 = (bf16[96,768]{1,0:T(8,128)(2,1)S(1)}, bf16[96,768]{1,0:T(8,128)(2,1)S(1)}, u32[]{:S(2)}, u32[]{:S(2)}) collective-permute-start(bf16[96,768]{1,0:T(8,128)(2,1)S(1)} %convert_bitcast_fusion), channel_id=1, source_target_pairs={{0,6},{1,7},{2,4},{3,5},{4,2},{5,3},{6,0},{7,1},{8,14},{9,15},{10,... | collective-permute-start | bytes 442376 | tf_op jit(solution)/shard_map/ppermute | solution.py:84
  26.4 1.7 collective-permute-start.8
  28.3 3.9 %collective-permute-done.10 = bf16[96,768]{1,0:T(8,128)(2,1)S(1)} collective-permute-done((bf16[96,768]{1,0:T(8,128)(2,1)S(1)}, bf16[96,768]{1,0:T(8,128)(2,1)S(1)}, u32[]{:S(2)}, u32[]{:S(2)}) %collective-permute-start.10) | collective-permute-done | bytes 147488 | tf_op jit(solution)/shard_map/ppermute | solution.py:84
  32.2 5.5 %collective-permute-done.9 = bf16[96,768]{1,0:T(8,128)(2,1)S(1)} collective-permute-done((bf16[96,768]{1,0:T(8,128)(2,1)S(1)}, bf16[96,768]{1,0:T(8,128)(2,1)S(1)}, u32[]{:S(2)}, u32[]{:S(2)}) %collective-permute-start.9) | collective-permute-done | bytes 147488 | tf_op jit(solution)/shard_map/ppermute | solution.py:84
  37.9 2.4 %shard_map.273 = (bf16[8,96,576]{2,1,0:T(8,128)(2,1)}, f32[8,12,96]{2,1,0:T(8,128)}) custom-call(s32[1]{0:T(128)} %bitcast.2.at_ref, bf16[4,112,576]{2,1,0:T(8,128)(2,1)} %copy-done.14, bf16[4,112,576]{2,1,0:T(8,128)(2,1)} %collective-permute-done.5.far_ref), custom_call_target="tpu_custom_call" | custom-call | tf_op jit(solution)/shard_map/pallas_call | solution.py:179
  41.2 7.8 %shard_map.274 = (bf16[512,768]{1,0:T(8,128)(2,1)}, bf16[512,768]{1,0:T(8,128)(2,1)}, bf16[512,576]{1,0:T(8,128)(2,1)}, f32[12,128,128]{2,1,0:T(8,128)}, bf16[4,...) custom-call(s32[1]{0:T(128)} %bitcast._.at_ref, bf16[2,272,768]{2,1,0:T(8,128)(2,1)} %copy-done.8, ...), custom_call_target="tpu_custom_call" | custom-call | tf_op jit(solution)/shard_map/pallas_call | solution.py:187
  51.7 2.3 shard_map.275
  56.3 3.9 %collective-permute-done.7 = bf16[1,2,128,192]{3,2,1,0:T(8,128)(2,1)S(1)} collective-permute-done((bf16[1,2,128,192]{3,2,1,0:T(8,128)(2,1)S(1)}, bf16[1,2,128,192]{3,2,1,0:T(8,128)(2,1)S(1)}, u32[]{:S(2)}, u32[]{:S(2)}) %collective-permute-start.7) | collective-permute-done | bytes 98336 | tf_op jit(solution)/shard_map/ppermute | solution.py:95
  62.9 3.3 %shard_map.276 = bf16[96,1536]{1,0:T(8,128)(2,1)} custom-call(s32[1]{0:T(128)} %bitcast._.at_ref, f32[96,3072]{1,0:T(8,128)} %bitcast.218, f32[384,768]{1,0:T(8,128)} %bitcast.219), custom_call_target="tpu_custom_call" | custom-call | tf_op jit(solution)/shard_map/pallas_call | solution.py:187
  66.3 2.3 collective-permute-start.15
  68.7 1.9 collective-permute-start.16
  70.6 8.0 %collective-permute-done.14 = bf16[96,1536]{1,0:T(8,128)(2,1)S(1)} collective-permute-done((bf16[96,1536]{1,0:T(8,128)(2,1)}, bf16[96,1536]{1,0:T(8,128)(2,1)S(1)}, u32[]{:S(2)}, u32[]{:S(2)}) %collective-permute-start.14) | collective-permute-done | bytes 294944 | tf_op jit(solution)/shard_map/ppermute | solution.py:84
  78.6 10.2 %collective-permute-done.15 = bf16[96,1536]{1,0:T(8,128)(2,1)S(1)} collective-permute-done((bf16[96,1536]{1,0:T(8,128)(2,1)}, bf16[96,1536]{1,0:T(8,128)(2,1)S(1)}, u32[]{:S(2)}, u32[]{:S(2)}) %collective-permute-start.15) | collective-permute-done | bytes 294944 | tf_op jit(solution)/shard_map/ppermute | solution.py:84
  92.8 5.1 %collective-permute-done.13 = bf16[2,128,768]{2,1,0:T(8,128)(2,1)S(1)} collective-permute-done((bf16[2,128,768]{2,1,0:T(8,128)(2,1)S(1)}, bf16[2,128,768]{2,1,0:T(8,128)(2,1)S(1)}, u32[]{:S(2)}, u32[]{:S(2)}) %collective-permute-start.13) | collective-permute-done | bytes 393248 | tf_op jit(solution)/shard_map/ppermute | solution.py:95
  98.2 3.2 %shard_map.277 = bf16[8,96,1536]{2,1,0:T(8,128)(2,1)} custom-call(s32[1]{0:T(128)} %bitcast.2.at_ref, bf16[4,96,1536]{2,1,0:T(8,128)(2,1)} %copy-done.6, bf16[4,96,1536]{2,1,0:T(8,128)(2,1)} %collective-permute-done.17.far_ref), custom_call_target="tpu_custom_call" | custom-call | tf_op jit(solution)/shard_map/pallas_call | solution.py:179
  101.4 2.2 convolution_add_fusion
  111.9 3.0 %collective-permute-done.18 = bf16[2,128,768]{2,1,0:T(8,128)(2,1)S(1)} collective-permute-done((bf16[2,128,768]{2,1,0:T(8,128)(2,1)S(1)}, bf16[2,128,768]{2,1,0:T(8,128)(2,1)S(1)}, u32[]{:S(2)}, u32[]{:S(2)}) %collective-permute-start.18) | collective-permute-done | bytes 393248 | tf_op jit(solution)/shard_map/ppermute | solution.py:95
  117.8 2.9 %collective-permute-done.19 = bf16[1,128,768]{2,1,0:T(8,128)(2,1)S(1)} collective-permute-done((bf16[1,128,768]{2,1,0:T(8,128)(2,1)S(1)}, bf16[1,128,768]{2,1,0:T(8,128)(2,1)S(1)}, u32[]{:S(2)}, u32[]{:S(2)}) %collective-permute-start.19) | collective-permute-done | bytes 196640 | tf_op jit(solution)/shard_map/ppermute | solution.py:95
  124.7 3.2 %collective-permute-done.20 = bf16[2,1,128,192]{3,2,0,1:T(8,128)(2,1)S(1)} collective-permute-done((bf16[2,1,128,192]{3,2,0,1:T(8,128)(2,1)S(1)}, bf16[2,1,128,192]{3,2,0,1:T(8,128)(2,1)S(1)}, u32[]{:S(2)}, u32[]{:S(2)}) %collective-permute-start.20) | collective-permute-done | bytes 98336 | tf_op jit(solution)/shard_map/ppermute | solution.py:95
  128.0 2.1 collective-permute-start.21
  130.8 2.3 collective-permute-done.21
  133.8 2.0 collective-permute-start.22
  135.9 8.2 %shard_map.278 = (f32[2,128,768]{2,1,0:T(8,128)}, bf16[2,128,768]{2,1,0:T(8,128)(2,1)}, f32[4,96,576]{2,1,0:T(8,128)}, bf16[4,96,576]{2,1,0:T(8,128)(2,1)}, f32[1,576]{1,0:T(1,128)}, /*index=5*/bf16[512,576]{1,0:T(8,128)(2,1)}) custom-call(s32[2]{0:T(128)} %pad_add_fusion.at_ref, bf16[512,576]{1,0:T(8,128)(2,1)} %get-tuple-element.54.packed_ref, ...), custom_call_target="tpu_custom_call" | custom-call | tf_op jit(solution)/shard_map/pallas_call | solution.py:187
  144.2 2.7 %fusion.57 = (bf16[4,96,768]{2,1,0:T(8,128)(2,1)S(1)}, f32[4,96,768]{2,1,0:T(8,128)}) fusion(bf16[4,96,768]{2,1,0:T(8,128)(2,1)} %collective-permute-done.38, f32[4,2,96,768]{3,2,1,0:T(8,128)} %bitcast.201, s32[]{:T(128)S(6)} %select_n.188), kind=kLoop, calls=%fused_computation.162 | loop fusion | flops 884736 | bytes 3538948 | tf_op jit(solution)/shard_map/convert_element_type | solution.py:384
  147.6 2.0 collective-permute-start.41
  149.6 3.3 %collective-permute-start.40 = (bf16[96,768]{1,0:T(8,128)(2,1)}, bf16[96,768]{1,0:T(8,128)(2,1)}, u32[]{:S(2)}, u32[]{:S(2)}) collective-permute-start(bf16[96,768]{1,0:T(8,128)(2,1)} %get-tuple-element.98), channel_id=1, source_target_pairs={{0,4},{1,5},{2,6},{3,7},{4,0},{5,1},{6,2},{7,3},{8,12},{9,13},{10,... | collective-permute-start | bytes 442376 | tf_op jit(solution)/shard_map/ppermute | solution.py:84
  155.6 2.2 collective-permute-start.25
  157.9 3.1 %fusion.55 = (bf16[4,96,1536]{2,1,0:T(8,128)(2,1)S(1)}, f32[4,96,1536]{2,1,0:T(8,128)}) fusion(bf16[4,96,1536]{2,1,0:T(8,128)(2,1)} %collective-permute-done.44, s32[]{:T(128)S(6)} %select_n.188, f32[4,2,96,768]{3,2,1,0:T(8,128)S(1)} %bitcast.199, f32[4,2,96,768]{3,2,1,0:T(8,128)S(1)} %fusion.20), kind=kLoop, calls=%fused_computation.161 | loop fusion | flops 2359296 | bytes 9437188 | tf_op jit(solution)/shard_map/convert_element_type | solution.py:384
  161.5 1.9 collective-permute-start.47
  164.2 2.5 %shard_map.279 = (f32[128,768]{1,0:T(8,128)}, f32[4,12,96]{2,1,0:T(8,128)}, bf16[4,12,96]{2,1,0:T(8,128)(2,1)}) custom-call(s32[2]{0:T(128)} %pad_add_fusion.at_ref, f32[128,768]{1,0:T(8,128)} %hidden_ref.3, f32[128,768]{1,0:T(8,128)} %fusion.26.grad_ref, f32[128,768]{1,0:T(8,128)} %copy-done.5, f32[1,768]{1,0:T(1,128)} %get-tuple-element.116.gain_ref, ...), custom_call_target="tpu_custom_call" | custom-call | tf_op jit(solution)/shard_map/pallas_call | solution.py:187
  168.2 2.0 collective-permute-start.29
  174.4 10.7 %collective-permute-start.27 = (bf16[12,96]{1,0:T(8,128)(2,1)S(1)}, bf16[12,96]{1,0:T(8,128)(2,1)S(1)}, u32[]{:S(2)}, u32[]{:S(2)}) collective-permute-start(bf16[12,96]{1,0:T(8,128)(2,1)S(1)} %get-tuple-element.117), channel_id=1, source_target_pairs={{0,2},{1,3},{2,0},{3,1},{4,6},{5,7},{6,4},{7,5},{8,10},{9,11},{10,... | collective-permute-start | bytes 6920 | tf_op jit(solution)/shard_map/ppermute | solution.py:84
  186.3 4.7 %collective-permute-done.28 = bf16[12,96]{1,0:T(8,128)(2,1)S(1)} collective-permute-done((bf16[12,96]{1,0:T(8,128)(2,1)S(1)}, bf16[12,96]{1,0:T(8,128)(2,1)S(1)}, u32[]{:S(2)}, u32[]{:S(2)}) %collective-permute-start.28) | collective-permute-done | bytes 2336 | tf_op jit(solution)/shard_map/ppermute | solution.py:84
  191.0 2.0 collective-permute-start.23
  194.5 2.9 %collective-permute-start.33 = (bf16[96,576]{1,0:T(8,128)(2,1)S(1)}, bf16[96,576]{1,0:T(8,128)(2,1)S(1)}, u32[]{:S(2)}, u32[]{:S(2)}) collective-permute-start(bf16[96,576]{1,0:T(8,128)(2,1)S(1)} %get-tuple-element.99), channel_id=1, source_target_pairs={{0,2},{1,3},{2,0},{3,1},{4,6},{5,7},{6,4},{7,5},{8,10},{9,11},{10,... | collective-permute-start | bytes 331784 | tf_op jit(solution)/shard_map/ppermute | solution.py:84
  198.7 2.4 collective-permute-done.35
  201.1 3.9 %collective-permute-done.34 = bf16[96,576]{1,0:T(8,128)(2,1)S(1)} collective-permute-done((bf16[96,576]{1,0:T(8,128)(2,1)S(1)}, bf16[96,576]{1,0:T(8,128)(2,1)S(1)}, u32[]{:S(2)}, u32[]{:S(2)}) %collective-permute-start.34) | collective-permute-done | bytes 110624 | tf_op jit(solution)/shard_map/ppermute | solution.py:84
  205.4 1.7 collective-permute-start.36
  207.6 4.2 %collective-permute-done.48 = bf16[1,96,1536]{2,1,0:T(8,128)(2,1)S(1)} collective-permute-done((bf16[1,96,1536]{2,1,0:T(8,128)(2,1)S(1)}, bf16[1,96,1536]{2,1,0:T(8,128)(2,1)S(1)}, u32[]{:S(2)}, u32[]{:S(2)}) %collective-permute-start.48) | collective-permute-done | bytes 294944 | tf_op jit(solution)/shard_map/ppermute | solution.py:95
  213.8 1.7 collective-permute-start.43
  217.5 10.2 %collective-permute-done.37.high_ref = bf16[2,96,576]{2,1,0:T(8,128)(2,1)S(1)} collective-permute-done((bf16[2,96,576]{2,1,0:T(8,128)(2,1)S(1)}, bf16[2,96,576]{2,1,0:T(8,128)(2,1)S(1)}, u32[]{:S(2)}, u32[]{:S(2)}) %collective-permute-start.37) | collective-permute-done | bytes 221216 | tf_op jit(solution)/shard_map/ppermute | solution.py:95
  228.3 2.3 shard_map.280
  232.2 3.4 %shard_map.281 = (f32[96,3072]{1,0:T(8,128)}, f32[384,768]{1,0:T(8,128)}) custom-call(s32[2]{0:T(128)} %pad_add_fusion.at_ref, bf16[2,96,1536]{2,1,0:T(8,128)(2,1)} %copy-done.13, bf16[2,96,1536]{2,1,0:T(8,128)(2,1)} %copy-done.28), custom_call_target="tpu_custom_call" | custom-call | tf_op jit(solution)/shard_map/pallas_call | solution.py:187
  (224 shorter events, 56.3 us)
Async XLA Ops:
  2.7 9.6 %collective-permute-start = (bf16[1,272,768]{2,1,0:T(8,128)(2,1)}, bf16[1,272,768]{2,1,0:T(8,128)(2,1)S(1)}, u32[]{:S(2)}, u32[]{:S(2)}) collective-permute-start(bf16[1,272,768]{2,1,0:T(8,128)(2,1)} %bitcast.213), channel_id=1, source_target_pairs={{0,8},{1,17},{2,10},{3,19},{4,12},{5,21},{6,14},{7,23},{8,0},{9,25... | collective-permute-start | bytes 1253384 | tf_op jit(solution)/shard_map/ppermute | solution.py:95
  8.0 8.7 %collective-permute-start.4 = (bf16[112,576]{1,0:T(8,128)(2,1)}, bf16[112,576]{1,0:T(8,128)(2,1)S(1)}, u32[]{:S(2)}, u32[]{:S(2)}) collective-permute-start(bf16[112,576]{1,0:T(8,128)(2,1)} %shard_map.272), channel_id=1, source_target_pairs={{0,6},{1,7},{2,4},{3,5},{4,2},{5,3},{6,0},{7,1},{8,14},{9,15},{10,... | collective-permute-start | bytes 387080 | tf_op jit(solution)/shard_map/ppermute | solution.py:84
  11.6 12.1 %collective-permute-start.3 = (bf16[112,576]{1,0:T(8,128)(2,1)}, bf16[112,576]{1,0:T(8,128)(2,1)S(1)}, u32[]{:S(2)}, u32[]{:S(2)}) collective-permute-start(bf16[112,576]{1,0:T(8,128)(2,1)} %shard_map.272), channel_id=1, source_target_pairs={{0,4},{1,5},{2,6},{3,7},{4,0},{5,1},{6,2},{7,3},{8,12},{9,13},{10,... | collective-permute-start | bytes 387080 | tf_op jit(solution)/shard_map/ppermute | solution.py:84
  11.6 12.1 %collective-permute-start.2 = (bf16[112,576]{1,0:T(8,128)(2,1)}, bf16[112,576]{1,0:T(8,128)(2,1)S(1)}, u32[]{:S(2)}, u32[]{:S(2)}) collective-permute-start(bf16[112,576]{1,0:T(8,128)(2,1)} %shard_map.272), channel_id=1, source_target_pairs={{0,2},{1,3},{2,0},{3,1},{4,6},{5,7},{6,4},{7,5},{8,10},{9,11},{10,... | collective-permute-start | bytes 387080 | tf_op jit(solution)/shard_map/ppermute | solution.py:84
  13.5 26.9 %collective-permute-start.1 = (bf16[2,272,768]{2,1,0:T(8,128)(2,1)S(1)}, bf16[2,272,768]{2,1,0:T(8,128)(2,1)S(1)}, u32[]{:S(2)}, u32[]{:S(2)}) collective-permute-start(bf16[2,272,768]{2,1,0:T(8,128)(2,1)S(1)} %pad_maximum_fusion.1.low_ref), channel_id=1, source_target_pairs={{0,16},{1,9},{2,18},{3,11},{4,20},{5,13},{6,22},{7,15},{8,24},{9,1... | collective-permute-start | bytes 2506760 | tf_op jit(solution)/shard_map/ppermute | solution.py:95
  23.7 8.5 %collective-permute-start.10 = (bf16[96,768]{1,0:T(8,128)(2,1)S(1)}, bf16[96,768]{1,0:T(8,128)(2,1)S(1)}, u32[]{:S(2)}, u32[]{:S(2)}) collective-permute-start(bf16[96,768]{1,0:T(8,128)(2,1)S(1)} %convert_bitcast_fusion), channel_id=1, source_target_pairs={{0,6},{1,7},{2,4},{3,5},{4,2},{5,3},{6,0},{7,1},{8,14},{9,15},{10,... | collective-permute-start | bytes 442376 | tf_op jit(solution)/shard_map/ppermute | solution.py:84
  26.4 11.3 %collective-permute-start.9 = (bf16[96,768]{1,0:T(8,128)(2,1)S(1)}, bf16[96,768]{1,0:T(8,128)(2,1)S(1)}, u32[]{:S(2)}, u32[]{:S(2)}) collective-permute-start(bf16[96,768]{1,0:T(8,128)(2,1)S(1)} %convert_bitcast_fusion), channel_id=1, source_target_pairs={{0,4},{1,5},{2,6},{3,7},{4,0},{5,1},{6,2},{7,3},{8,12},{9,13},{10,... | collective-permute-start | bytes 442376 | tf_op jit(solution)/shard_map/ppermute | solution.py:84
  26.4 11.3 %collective-permute-start.8 = (bf16[96,768]{1,0:T(8,128)(2,1)S(1)}, bf16[96,768]{1,0:T(8,128)(2,1)S(1)}, u32[]{:S(2)}, u32[]{:S(2)}) collective-permute-start(bf16[96,768]{1,0:T(8,128)(2,1)S(1)} %convert_bitcast_fusion), channel_id=1, source_target_pairs={{0,2},{1,3},{2,0},{3,1},{4,6},{5,7},{6,4},{7,5},{8,10},{9,11},{10,... | collective-permute-start | bytes 442376 | tf_op jit(solution)/shard_map/ppermute | solution.py:84
  28.2 9.7 %collective-permute-start.5 = (bf16[4,112,576]{2,1,0:T(8,128)(2,1)S(1)}, bf16[4,112,576]{2,1,0:T(8,128)(2,1)}, u32[]{:S(2)}, u32[]{:S(2)}) collective-permute-start(bf16[4,112,576]{2,1,0:T(8,128)(2,1)S(1)} %pad_maximum_fusion.5.near_ref), channel_id=1, source_target_pairs={{0,1},{1,0},{2,3},{3,2},{4,5},{5,4},{6,7},{7,6},{8,9},{9,8},{10,11... | collective-permute-start | bytes 1548296 | tf_op jit(solution)/shard_map/ppermute | solution.py:84
  37.8 13.8 %collective-permute-start.11 = (bf16[4,96,768]{2,1,0:T(8,128)(2,1)S(1)}, bf16[4,96,768]{2,1,0:T(8,128)(2,1)}, u32[]{:S(2)}, u32[]{:S(2)}) collective-permute-start(bf16[4,96,768]{2,1,0:T(8,128)(2,1)S(1)} %pad_maximum_fusion.3.near_ref), channel_id=1, source_target_pairs={{0,1},{1,0},{2,3},{3,2},{4,5},{5,4},{6,7},{7,6},{8,9},{9,8},{10,11... | collective-permute-start | bytes 1769480 | tf_op jit(solution)/shard_map/ppermute | solution.py:84
  50.0 5.0 %collective-permute-start.6 = (bf16[2,1,128,192]{3,2,0,1:T(8,128)(2,1)S(1)}, bf16[2,1,128,192]{3,2,0,1:T(8,128)(2,1)S(1)}, u32[]{:S(2)}, u32[]{:S(2)}) collective-permute-start(bf16[2,1,128,192]{3,2,0,1:T(8,128)(2,1)S(1)} %get-tuple-element.113), channel_id=1, source_target_pairs={{0,8},{1,17},{2,10},{3,19},{4,12},{5,21},{6,14},{7,23},{8,0},{9,25... | collective-permute-start | bytes 294920 | tf_op jit(solution)/shard_map/ppermute | solution.py:95
  55.1 5.0 %collective-permute-start.7 = (bf16[1,2,128,192]{3,2,1,0:T(8,128)(2,1)S(1)}, bf16[1,2,128,192]{3,2,1,0:T(8,128)(2,1)S(1)}, u32[]{:S(2)}, u32[]{:S(2)}) collective-permute-start(bf16[1,2,128,192]{3,2,1,0:T(8,128)(2,1)S(1)} %get-tuple-element.111), channel_id=1, source_target_pairs={{0,16},{1,9},{2,18},{3,11},{4,20},{5,13},{6,22},{7,15},{8,24},{9,1... | collective-permute-start | bytes 294920 | tf_op jit(solution)/shard_map/ppermute | solution.py:95
  61.2 9.3 %collective-permute-start.12 = (bf16[1,128,768]{2,1,0:T(8,128)(2,1)S(1)}, bf16[1,128,768]{2,1,0:T(8,128)(2,1)S(1)}, u32[]{:S(2)}, u32[]{:S(2)}) collective-permute-start(bf16[1,128,768]{2,1,0:T(8,128)(2,1)S(1)} %fusion.38), channel_id=1, source_target_pairs={{0,8},{1,17},{2,10},{3,19},{4,12},{5,21},{6,14},{7,23},{8,0},{9,25... | collective-permute-start | bytes 589832 | tf_op jit(solution)/shard_map/ppermute | solution.py:95
  66.2 12.4 %collective-permute-start.14 = (bf16[96,1536]{1,0:T(8,128)(2,1)}, bf16[96,1536]{1,0:T(8,128)(2,1)S(1)}, u32[]{:S(2)}, u32[]{:S(2)}) collective-permute-start(bf16[96,1536]{1,0:T(8,128)(2,1)} %shard_map.276), channel_id=1, source_target_pairs={{0,2},{1,3},{2,0},{3,1},{4,6},{5,7},{6,4},{7,5},{8,10},{9,11},{10,... | collective-permute-start | bytes 884744 | tf_op jit(solution)/shard_map/ppermute | solution.py:84
  66.3 22.5 %collective-permute-start.15 = (bf16[96,1536]{1,0:T(8,128)(2,1)}, bf16[96,1536]{1,0:T(8,128)(2,1)S(1)}, u32[]{:S(2)}, u32[]{:S(2)}) collective-permute-start(bf16[96,1536]{1,0:T(8,128)(2,1)} %shard_map.276), channel_id=1, source_target_pairs={{0,4},{1,5},{2,6},{3,7},{4,0},{5,1},{6,2},{7,3},{8,12},{9,13},{10,... | collective-permute-start | bytes 884744 | tf_op jit(solution)/shard_map/ppermute | solution.py:84
  68.7 20.1 %collective-permute-start.16 = (bf16[96,1536]{1,0:T(8,128)(2,1)}, bf16[96,1536]{1,0:T(8,128)(2,1)S(1)}, u32[]{:S(2)}, u32[]{:S(2)}) collective-permute-start(bf16[96,1536]{1,0:T(8,128)(2,1)} %shard_map.276), channel_id=1, source_target_pairs={{0,6},{1,7},{2,4},{3,5},{4,2},{5,3},{6,0},{7,1},{8,14},{9,15},{10,... | collective-permute-start | bytes 884744 | tf_op jit(solution)/shard_map/ppermute | solution.py:84
  89.9 8.3 %collective-permute-start.17 = (bf16[4,96,1536]{2,1,0:T(8,128)(2,1)S(1)}, bf16[4,96,1536]{2,1,0:T(8,128)(2,1)}, u32[]{:S(2)}, u32[]{:S(2)}) collective-permute-start(bf16[4,96,1536]{2,1,0:T(8,128)(2,1)S(1)} %pad_maximum_fusion.near_ref), channel_id=1, source_target_pairs={{0,1},{1,0},{2,3},{3,2},{4,5},{5,4},{6,7},{7,6},{8,9},{9,8},{10,11... | collective-permute-start | bytes 3538952 | tf_op jit(solution)/shard_map/ppermute | solution.py:84
  90.0 7.8 %collective-permute-start.13 = (bf16[2,128,768]{2,1,0:T(8,128)(2,1)S(1)}, bf16[2,128,768]{2,1,0:T(8,128)(2,1)S(1)}, u32[]{:S(2)}, u32[]{:S(2)}) collective-permute-start(bf16[2,128,768]{2,1,0:T(8,128)(2,1)S(1)} %pad_maximum_fusion.6), channel_id=1, source_target_pairs={{0,16},{1,9},{2,18},{3,11},{4,20},{5,13},{6,22},{7,15},{8,24},{9,1... | collective-permute-start | bytes 1179656 | tf_op jit(solution)/shard_map/ppermute | solution.py:95
  107.1 7.8 %collective-permute-start.18 = (bf16[2,128,768]{2,1,0:T(8,128)(2,1)S(1)}, bf16[2,128,768]{2,1,0:T(8,128)(2,1)S(1)}, u32[]{:S(2)}, u32[]{:S(2)}) collective-permute-start(bf16[2,128,768]{2,1,0:T(8,128)(2,1)S(1)} %bitcast.226), channel_id=1, source_target_pairs={{0,16},{1,9},{2,18},{3,11},{4,20},{5,13},{6,22},{7,15},{8,24},{9,1... | collective-permute-start | bytes 1179656 | tf_op jit(solution)/shard_map/ppermute | solution.py:95
  115.0 5.7 %collective-permute-start.19 = (bf16[1,128,768]{2,1,0:T(8,128)(2,1)S(1)}, bf16[1,128,768]{2,1,0:T(8,128)(2,1)S(1)}, u32[]{:S(2)}, u32[]{:S(2)}) collective-permute-start(bf16[1,128,768]{2,1,0:T(8,128)(2,1)S(1)} %slice.303), channel_id=1, source_target_pairs={{0,8},{1,17},{2,10},{3,19},{4,12},{5,21},{6,14},{7,23},{8,0},{9,25... | collective-permute-start | bytes 589832 | tf_op jit(solution)/shard_map/ppermute | solution.py:95
  117.8 37.8 %collective-permute-start.44 = (bf16[4,96,1536]{2,1,0:T(8,128)(2,1)}, bf16[4,96,1536]{2,1,0:T(8,128)(2,1)}, u32[]{:S(2)}, u32[]{:S(2)}) collective-permute-start(bf16[4,96,1536]{2,1,0:T(8,128)(2,1)} %fusion.13), channel_id=1, source_target_pairs={{0,1},{1,0},{2,3},{3,2},{4,5},{5,4},{6,7},{7,6},{8,9},{9,8},{10,11... | collective-permute-start | bytes 3538952 | tf_op jit(solution)/shard_map/ppermute | solution.py:84
  124.5 19.6 %collective-permute-start.38 = (bf16[4,96,768]{2,1,0:T(8,128)(2,1)S(1)}, bf16[4,96,768]{2,1,0:T(8,128)(2,1)}, u32[]{:S(2)}, u32[]{:S(2)}) collective-permute-start(bf16[4,96,768]{2,1,0:T(8,128)(2,1)S(1)} %fusion.22), channel_id=1, source_target_pairs={{0,1},{1,0},{2,3},{3,2},{4,5},{5,4},{6,7},{7,6},{8,9},{9,8},{10,11... | collective-permute-start | bytes 1769480 | tf_op jit(solution)/shard_map/ppermute | solution.py:84
  128.0 5.1 %collective-permute-start.21 = (bf16[1,2,128,192]{3,2,1,0:T(8,128)(2,1)S(1)}, bf16[1,2,128,192]{3,2,1,0:T(8,128)(2,1)S(1)}, u32[]{:S(2)}, u32[]{:S(2)}) collective-permute-start(bf16[1,2,128,192]{3,2,1,0:T(8,128)(2,1)S(1)} %get-tuple-element.107), channel_id=1, source_target_pairs={{0,16},{1,9},{2,18},{3,11},{4,20},{5,13},{6,22},{7,15},{8,24},{9,1... | collective-permute-start | bytes 294920 | tf_op jit(solution)/shard_map/ppermute | solution.py:95
  133.8 15.8 %collective-permute-start.22 = (bf16[2,128,768]{2,1,0:T(8,128)(2,1)}, bf16[2,128,768]{2,1,0:T(8,128)(2,1)}, u32[]{:S(2)}, u32[]{:S(2)}) collective-permute-start(bf16[2,128,768]{2,1,0:T(8,128)(2,1)} %bitcast.36), channel_id=1, source_target_pairs={{0,16},{1,9},{2,18},{3,11},{4,20},{5,13},{6,22},{7,15},{8,24},{9,1... | collective-permute-start | bytes 1179656 | tf_op jit(solution)/shard_map/ppermute | solution.py:95
  144.1 10.7 %collective-permute-start.24 = (bf16[2,128,768]{2,1,0:T(8,128)(2,1)}, bf16[2,128,768]{2,1,0:T(8,128)(2,1)S(1)}, u32[]{:S(2)}, u32[]{:S(2)}) collective-permute-start(bf16[2,128,768]{2,1,0:T(8,128)(2,1)} %get-tuple-element.58), channel_id=1, source_target_pairs={{0,16},{1,9},{2,18},{3,11},{4,20},{5,13},{6,22},{7,15},{8,24},{9,1... | collective-permute-start | bytes 1179656 | tf_op jit(solution)/shard_map/ppermute | solution.py:95
  144.1 22.6 %collective-permute-start.32 = (bf16[4,96,576]{2,1,0:T(8,128)(2,1)}, bf16[4,96,576]{2,1,0:T(8,128)(2,1)}, u32[]{:S(2)}, u32[]{:S(2)}) collective-permute-start(bf16[4,96,576]{2,1,0:T(8,128)(2,1)} %get-tuple-element.64), channel_id=1, source_target_pairs={{0,1},{1,0},{2,3},{3,2},{4,5},{5,4},{6,7},{7,6},{8,9},{9,8},{10,11... | collective-permute-start | bytes 1327112 | tf_op jit(solution)/shard_map/ppermute | solution.py:84
  147.6 22.6 %collective-permute-start.41 = (bf16[96,768]{1,0:T(8,128)(2,1)}, bf16[96,768]{1,0:T(8,128)(2,1)}, u32[]{:S(2)}, u32[]{:S(2)}) collective-permute-start(bf16[96,768]{1,0:T(8,128)(2,1)} %get-tuple-element.97), channel_id=1, source_target_pairs={{0,6},{1,7},{2,4},{3,5},{4,2},{5,3},{6,0},{7,1},{8,14},{9,15},{10,... | collective-permute-start | bytes 442376 | tf_op jit(solution)/shard_map/ppermute | solution.py:84
  149.6 22.1 %collective-permute-start.40 = (bf16[96,768]{1,0:T(8,128)(2,1)}, bf16[96,768]{1,0:T(8,128)(2,1)}, u32[]{:S(2)}, u32[]{:S(2)}) collective-permute-start(bf16[96,768]{1,0:T(8,128)(2,1)} %get-tuple-element.98), channel_id=1, source_target_pairs={{0,4},{1,5},{2,6},{3,7},{4,0},{5,1},{6,2},{7,3},{8,12},{9,13},{10,... | collective-permute-start | bytes 442376 | tf_op jit(solution)/shard_map/ppermute | solution.py:84
  154.8 18.0 %collective-permute-start.39 = (bf16[96,768]{1,0:T(8,128)(2,1)}, bf16[96,768]{1,0:T(8,128)(2,1)}, u32[]{:S(2)}, u32[]{:S(2)}) collective-permute-start(bf16[96,768]{1,0:T(8,128)(2,1)} %get-tuple-element.96), channel_id=1, source_target_pairs={{0,2},{1,3},{2,0},{3,1},{4,6},{5,7},{6,4},{7,5},{8,10},{9,11},{10,... | collective-permute-start | bytes 442376 | tf_op jit(solution)/shard_map/ppermute | solution.py:84
  155.6 5.9 %collective-permute-start.25 = (bf16[1,128,768]{2,1,0:T(8,128)(2,1)S(1)}, bf16[1,128,768]{2,1,0:T(8,128)(2,1)S(1)}, u32[]{:S(2)}, u32[]{:S(2)}) collective-permute-start(bf16[1,128,768]{2,1,0:T(8,128)(2,1)S(1)} %slice.301), channel_id=1, source_target_pairs={{0,8},{1,17},{2,10},{3,19},{4,12},{5,21},{6,14},{7,23},{8,0},{9,25... | collective-permute-start | bytes 589832 | tf_op jit(solution)/shard_map/ppermute | solution.py:95
  161.5 32.9 %collective-permute-start.47 = (bf16[96,1536]{1,0:T(8,128)(2,1)S(1)}, bf16[96,1536]{1,0:T(8,128)(2,1)S(1)}, u32[]{:S(2)}, u32[]{:S(2)}) collective-permute-start(bf16[96,1536]{1,0:T(8,128)(2,1)S(1)} %get-tuple-element.94), channel_id=1, source_target_pairs={{0,6},{1,7},{2,4},{3,5},{4,2},{5,3},{6,0},{7,1},{8,14},{9,15},{10,... | collective-permute-start | bytes 884744 | tf_op jit(solution)/shard_map/ppermute | solution.py:84
  168.2 6.2 %collective-permute-start.29 = (bf16[12,96]{1,0:T(8,128)(2,1)S(1)}, bf16[12,96]{1,0:T(8,128)(2,1)S(1)}, u32[]{:S(2)}, u32[]{:S(2)}) collective-permute-start(bf16[12,96]{1,0:T(8,128)(2,1)S(1)} %get-tuple-element.118), channel_id=1, source_target_pairs={{0,6},{1,7},{2,4},{3,5},{4,2},{5,3},{6,0},{7,1},{8,14},{9,15},{10,... | collective-permute-start | bytes 6920 | tf_op jit(solution)/shard_map/ppermute | solution.py:84
  170.2 24.3 %collective-permute-start.46 = (bf16[96,1536]{1,0:T(8,128)(2,1)S(1)}, bf16[96,1536]{1,0:T(8,128)(2,1)S(1)}, u32[]{:S(2)}, u32[]{:S(2)}) collective-permute-start(bf16[96,1536]{1,0:T(8,128)(2,1)S(1)} %get-tuple-element.95), channel_id=1, source_target_pairs={{0,4},{1,5},{2,6},{3,7},{4,0},{5,1},{6,2},{7,3},{8,12},{9,13},{10,... | collective-permute-start | bytes 884744 | tf_op jit(solution)/shard_map/ppermute | solution.py:84
  171.8 25.7 %collective-permute-start.45 = (bf16[96,1536]{1,0:T(8,128)(2,1)S(1)}, bf16[96,1536]{1,0:T(8,128)(2,1)S(1)}, u32[]{:S(2)}, u32[]{:S(2)}) collective-permute-start(bf16[96,1536]{1,0:T(8,128)(2,1)S(1)} %get-tuple-element.93), channel_id=1, source_target_pairs={{0,2},{1,3},{2,0},{3,1},{4,6},{5,7},{6,4},{7,5},{8,10},{9,11},{10,... | collective-permute-start | bytes 884744 | tf_op jit(solution)/shard_map/ppermute | solution.py:84
  172.8 18.2 %collective-permute-start.28 = (bf16[12,96]{1,0:T(8,128)(2,1)S(1)}, bf16[12,96]{1,0:T(8,128)(2,1)S(1)}, u32[]{:S(2)}, u32[]{:S(2)}) collective-permute-start(bf16[12,96]{1,0:T(8,128)(2,1)S(1)} %get-tuple-element.119), channel_id=1, source_target_pairs={{0,4},{1,5},{2,6},{3,7},{4,0},{5,1},{6,2},{7,3},{8,12},{9,13},{10,... | collective-permute-start | bytes 6920 | tf_op jit(solution)/shard_map/ppermute | solution.py:84
  174.4 18.6 %collective-permute-start.27 = (bf16[12,96]{1,0:T(8,128)(2,1)S(1)}, bf16[12,96]{1,0:T(8,128)(2,1)S(1)}, u32[]{:S(2)}, u32[]{:S(2)}) collective-permute-start(bf16[12,96]{1,0:T(8,128)(2,1)S(1)} %get-tuple-element.117), channel_id=1, source_target_pairs={{0,2},{1,3},{2,0},{3,1},{4,6},{5,7},{6,4},{7,5},{8,10},{9,11},{10,... | collective-permute-start | bytes 6920 | tf_op jit(solution)/shard_map/ppermute | solution.py:84
  191.0 21.3 %collective-permute-start.23 = (bf16[1,128,768]{2,1,0:T(8,128)(2,1)S(1)}, bf16[1,128,768]{2,1,0:T(8,128)(2,1)S(1)}, u32[]{:S(2)}, u32[]{:S(2)}) collective-permute-start(bf16[1,128,768]{2,1,0:T(8,128)(2,1)S(1)} %copy-done.32), channel_id=1, source_target_pairs={{0,8},{1,17},{2,10},{3,19},{4,12},{5,21},{6,14},{7,23},{8,0},{9,25... | collective-permute-start | bytes 589832 | tf_op jit(solution)/shard_map/ppermute | solution.py:95
  192.9 8.1 %collective-permute-start.35 = (bf16[96,576]{1,0:T(8,128)(2,1)S(1)}, bf16[96,576]{1,0:T(8,128)(2,1)S(1)}, u32[]{:S(2)}, u32[]{:S(2)}) collective-permute-start(bf16[96,576]{1,0:T(8,128)(2,1)S(1)} %get-tuple-element.100), channel_id=1, source_target_pairs={{0,6},{1,7},{2,4},{3,5},{4,2},{5,3},{6,0},{7,1},{8,14},{9,15},{10,... | collective-permute-start | bytes 331784 | tf_op jit(solution)/shard_map/ppermute | solution.py:84
  194.4 10.5 %collective-permute-start.34 = (bf16[96,576]{1,0:T(8,128)(2,1)S(1)}, bf16[96,576]{1,0:T(8,128)(2,1)S(1)}, u32[]{:S(2)}, u32[]{:S(2)}) collective-permute-start(bf16[96,576]{1,0:T(8,128)(2,1)S(1)} %get-tuple-element.101), channel_id=1, source_target_pairs={{0,4},{1,5},{2,6},{3,7},{4,0},{5,1},{6,2},{7,3},{8,12},{9,13},{10,... | collective-permute-start | bytes 331784 | tf_op jit(solution)/shard_map/ppermute | solution.py:84
  194.5 10.8 %collective-permute-start.33 = (bf16[96,576]{1,0:T(8,128)(2,1)S(1)}, bf16[96,576]{1,0:T(8,128)(2,1)S(1)}, u32[]{:S(2)}, u32[]{:S(2)}) collective-permute-start(bf16[96,576]{1,0:T(8,128)(2,1)S(1)} %get-tuple-element.99), channel_id=1, source_target_pairs={{0,2},{1,3},{2,0},{3,1},{4,6},{5,7},{6,4},{7,5},{8,10},{9,11},{10,... | collective-permute-start | bytes 331784 | tf_op jit(solution)/shard_map/ppermute | solution.py:84
  197.4 16.3 %collective-permute-start.42 = (bf16[1,96,768]{2,1,0:T(8,128)(2,1)S(1)}, bf16[1,96,768]{2,1,0:T(8,128)(2,1)S(1)}, u32[]{:S(2)}, u32[]{:S(2)}) collective-permute-start(bf16[1,96,768]{2,1,0:T(8,128)(2,1)S(1)} %fusion.39), channel_id=1, source_target_pairs={{0,8},{1,17},{2,10},{3,19},{4,12},{5,21},{6,14},{7,23},{8,0},{9,25... | collective-permute-start | bytes 442376 | tf_op jit(solution)/shard_map/ppermute | solution.py:95
  201.0 6.1 %collective-permute-start.30 = (bf16[1,12,96]{2,1,0:T(8,128)(2,1)S(1)}, bf16[1,12,96]{2,1,0:T(8,128)(2,1)S(1)}, u32[]{:S(2)}, u32[]{:S(2)}) collective-permute-start(bf16[1,12,96]{2,1,0:T(8,128)(2,1)S(1)} %fusion.47), channel_id=1, source_target_pairs={{0,8},{1,17},{2,10},{3,19},{4,12},{5,21},{6,14},{7,23},{8,0},{9,25... | collective-permute-start | bytes 6920 | tf_op jit(solution)/shard_map/ppermute | solution.py:95
  205.0 6.8 %collective-permute-start.48 = (bf16[1,96,1536]{2,1,0:T(8,128)(2,1)S(1)}, bf16[1,96,1536]{2,1,0:T(8,128)(2,1)S(1)}, u32[]{:S(2)}, u32[]{:S(2)}) collective-permute-start(bf16[1,96,1536]{2,1,0:T(8,128)(2,1)S(1)} %fusion.31), channel_id=1, source_target_pairs={{0,8},{1,17},{2,10},{3,19},{4,12},{5,21},{6,14},{7,23},{8,0},{9,25... | collective-permute-start | bytes 884744 | tf_op jit(solution)/shard_map/ppermute | solution.py:95
  205.4 10.1 %collective-permute-start.36 = (bf16[1,96,576]{2,1,0:T(8,128)(2,1)S(1)}, bf16[1,96,576]{2,1,0:T(8,128)(2,1)}, u32[]{:S(2)}, u32[]{:S(2)}) collective-permute-start(bf16[1,96,576]{2,1,0:T(8,128)(2,1)S(1)} %fusion.40), channel_id=1, source_target_pairs={{0,8},{1,17},{2,10},{3,19},{4,12},{5,21},{6,14},{7,23},{8,0},{9,25... | collective-permute-start | bytes 331784 | tf_op jit(solution)/shard_map/ppermute | solution.py:95
  207.2 5.9 %collective-permute-start.31 = (bf16[2,12,96]{2,1,0:T(8,128)(2,1)S(1)}, bf16[2,12,96]{2,1,0:T(8,128)(2,1)S(1)}, u32[]{:S(2)}, u32[]{:S(2)}) collective-permute-start(bf16[2,12,96]{2,1,0:T(8,128)(2,1)S(1)} %pad_maximum_fusion.14), channel_id=1, source_target_pairs={{0,16},{1,9},{2,18},{3,11},{4,20},{5,13},{6,22},{7,15},{8,24},{9,1... | collective-permute-start | bytes 13832 | tf_op jit(solution)/shard_map/ppermute | solution.py:95
  211.9 19.5 %collective-permute-start.49 = (bf16[2,96,1536]{2,1,0:T(8,128)(2,1)S(1)}, bf16[2,96,1536]{2,1,0:T(8,128)(2,1)S(1)}, u32[]{:S(2)}, u32[]{:S(2)}) collective-permute-start(bf16[2,96,1536]{2,1,0:T(8,128)(2,1)S(1)} %pad_maximum_fusion.4.low_ref), channel_id=1, source_target_pairs={{0,16},{1,9},{2,18},{3,11},{4,20},{5,13},{6,22},{7,15},{8,24},{9,1... | collective-permute-start | bytes 1769480 | tf_op jit(solution)/shard_map/ppermute | solution.py:95
  213.8 16.8 %collective-permute-start.43 = (bf16[2,96,768]{2,1,0:T(8,128)(2,1)S(1)}, bf16[2,96,768]{2,1,0:T(8,128)(2,1)S(1)}, u32[]{:S(2)}, u32[]{:S(2)}) collective-permute-start(bf16[2,96,768]{2,1,0:T(8,128)(2,1)S(1)} %pad_maximum_fusion.7), channel_id=1, source_target_pairs={{0,16},{1,9},{2,18},{3,11},{4,20},{5,13},{6,22},{7,15},{8,24},{9,1... | collective-permute-start | bytes 884744 | tf_op jit(solution)/shard_map/ppermute | solution.py:95
  216.5 11.1 %collective-permute-start.37 = (bf16[2,96,576]{2,1,0:T(8,128)(2,1)S(1)}, bf16[2,96,576]{2,1,0:T(8,128)(2,1)S(1)}, u32[]{:S(2)}, u32[]{:S(2)}) collective-permute-start(bf16[2,96,576]{2,1,0:T(8,128)(2,1)S(1)} %pad_maximum_fusion.11.low_ref), channel_id=1, source_target_pairs={{0,16},{1,9},{2,18},{3,11},{4,20},{5,13},{6,22},{7,15},{8,24},{9,1... | collective-permute-start | bytes 663560 | tf_op jit(solution)/shard_map/ppermute | solution.py:95
  (42 other events, 264.5 us)
